TPU v7x, 32 devices: a whole 2x2x4 slice. The times are simulated.
32 devices in a mesh: sec: 2 (over x), col: 2 (over y), elem: 8 (over z, core).
Axes of the slice: x: 2, y: 2, z: 4, core: 2. Of those that a mesh axis runs over, the one named last changes fastest.
Arguments:
- probes: float32 [64, 48, 256], P('col', 'elem'), may hold values from -6 to 6
- jacobian: float32 [2, 48, 7, 256, 256], P('sec', 'elem'), may hold values from -0.0625 to 0.0625
- neighbors: int32 [48, 7], P('elem'), may hold values from 0 to 47, as said below
- stations: int32 [512], P('elem'), may hold values from 0 to 47, as said below
- obs_weights: float32 [512, 256], P('elem'), may hold values from -0.75 to 0.75
Outputs:
- hess_probes: float32 [64, 48, 256], P('col', 'elem', 'sec')
- gram: float32 [64, 64], P('col')
Inputs may be any that keep to these rules, and one draw needn't show every extreme that they name: `neighbors`: row e lists the 7 elements e - 3 to e + 3, taken modulo 48, each once, in an order drawn for each row. Station i lies in one of the 6 elements from (i // 64) * 6 on; every element holds one or more stations.
All inputs are finite; a program needn't handle non-finite values.
Results may differ from a plain program's by a relative error of at most 0.0001.
Values sent between devices are 32-bit elements; how exact they have to be, the bound alone decides.
A program may use at most 64 MiB of HBM per device.

v0:
```python
import jax
import jax.numpy as jnp
from jax import lax
from jax.sharding import PartitionSpec as P

NBRS = 7
STEPS = 2


PRECISE = lax.Precision.HIGHEST


def with_halo(shard, sides, width):
    for axis, dim in sides:
        devices, length = (lax.axis_size(axis), shard.shape[dim])
        up = [(i, (i + 1) % devices) for i in range(devices)]
        down = [(j, i) for i, j in up]
        last = lax.slice_in_dim(shard, length - width, length, axis=dim)
        leading = lax.slice_in_dim(shard, 0, width, axis=dim)
        before = lax.ppermute(last, axis, up)
        after = lax.ppermute(leading, axis, down)
        shard = jnp.concatenate([before, shard, after], axis=dim)
    return shard


def from_behind(value, axis, steps):
    count = lax.axis_size(axis)
    pairs = [(source, (source + steps) % count) for source in range(count)]
    return lax.ppermute(value, axis, pairs)


def from_behind_2(value, axis, steps):
    count = lax.axis_size(axis)
    leading, last = (max(0, -steps), min(count, count - steps))
    return lax.ppermute(value, axis, [(source, source + steps) for source in range(leading, last)])


def tangent_pass(vector, blocks, lookup, radius):
    column_count, elem_count, dof_count = vector.shape
    for repeat in range(STEPS):
        extended = with_halo(vector, (("elem", 1),), radius)
        gathered = jnp.take(extended, lookup, axis=1).reshape(
            column_count, elem_count, NBRS, dof_count
        )
        vector = vector + jnp.einsum("cekI,ekJI->ceJ", gathered, blocks, precision=PRECISE)
    return vector


def adjoint_pass(vector, blocks, scatter_table, radius):
    column_count, elem_count, dof_count = vector.shape
    for repeat in range(STEPS):
        products = jnp.einsum("ceJ,ekJI->cekI", vector, blocks, precision=PRECISE)
        flattened = products.reshape(column_count, elem_count * NBRS, dof_count)
        extended = jnp.einsum("cxI,xy->cyI", flattened, scatter_table, precision=PRECISE)
        left_rim = extended[:, :radius]
        right_rim = extended[:, elem_count + radius :]
        from_right = from_behind(left_rim, "elem", -1)
        from_left = from_behind(right_rim, "elem", 1)
        centre = extended[:, radius : radius + elem_count]
        centre = centre.at[:, :radius].add(from_left)
        centre = centre.at[:, elem_count - radius :].add(from_right)
        vector = vector + centre
    return vector


def observe(vector, station_table, obs_weights):
    sampled = jnp.einsum("se,ceI->csI", station_table, vector, precision=PRECISE)
    readings = jnp.einsum("csI,sI->cs", sampled, obs_weights, precision=PRECISE)
    weighted = readings[:, :, None] * obs_weights[None, :, :]
    return jnp.einsum("csI,se->ceI", weighted, station_table, precision=PRECISE)


def per_device(probes, jacobian, neighbors, stations, obs_weights):
    column_count, elem_count, dof_count = probes.shape
    radius = (NBRS - 1) // 2
    elem_total = elem_count * lax.axis_size("elem")
    first_elem = lax.axis_index("elem") * elem_count
    lookup = ((neighbors - first_elem + radius) % elem_total).reshape(-1)
    ext_ids = jnp.arange(elem_count + 2 * radius, dtype=jnp.int32)
    scatter_table = (lookup[:, None] == ext_ids[None, :]).astype(jnp.float32)
    local_ids = jnp.arange(elem_count, dtype=jnp.int32)
    station_table = ((stations - first_elem)[:, None] == local_ids[None, :]).astype(jnp.float32)
    segment_index = lax.axis_index("sec")
    leading = segment_index == 0
    half_order = dof_count // 2
    blocks = jacobian[0]
    batch_count = 1
    batch_list = [probes]
    rounds = batch_count + 1
    stored = []
    incoming = jnp.zeros_like(batch_list[0])
    for round_number in range(rounds):
        start_vector = batch_list[min(round_number, batch_count - 1)]
        inputs = jnp.where(leading, start_vector, incoming)
        output = tangent_pass(inputs, blocks, lookup, radius)
        stored.append(output)
        if round_number + 1 < rounds:
            incoming = from_behind_2(output, "sec", 1)
    results = []
    returning = jnp.zeros_like(batch_list[0])
    for round_number in range(rounds):
        state_now = jnp.where(
            leading, stored[max(round_number - 1, 0)], stored[min(round_number + 1, rounds - 1)]
        )
        inputs = returning + observe(state_now, station_table, obs_weights)
        output = adjoint_pass(inputs, blocks, scatter_table, radius)
        if round_number >= 1:
            results.append(output)
        if round_number + 1 < rounds:
            returning = from_behind_2(output, "sec", -1)
    hessian_all = results[0]
    upper_half = from_behind_2(hessian_all[:, :, half_order:], "sec", 1)
    hess_local = jnp.where(leading, hessian_all[:, :, :half_order], upper_half)
    probe_half = lax.dynamic_slice_in_dim(probes, segment_index * half_order, half_order, 2)
    scaling = 1.0 / (elem_total * dof_count)
    shard_piece = lax.all_gather(probe_half, "col", axis=0, tiled=True)
    flat_piece = shard_piece.reshape(shard_piece.shape[0], -1)
    partial_gram = jnp.einsum(
        "ax,bx->ab", hess_local.reshape(column_count, -1), flat_piece, precision=PRECISE
    )
    gram = lax.psum(partial_gram, ("sec", "elem")) * scaling
    return (hess_local, gram)


def solution(mesh):
    in_specs = (
        P("col", "elem", None),
        P("sec", "elem", None, None, None),
        P("elem", None),
        P("elem"),
        P("elem", None),
    )
    out_specs = (P("col", "elem", "sec"), P("col", None))
    return jax.shard_map(
        per_device, mesh=mesh, in_specs=in_specs, out_specs=out_specs, check_vma=False
    )
```

profile of v0, /device:TPU:0, one launch (start us, length us, event | category | flops | bytes accessed | tf_op | source)
XLA Modules:
  0.0 249.6 jit_solution(15694952835466380910)
XLA Ops:
  2.2 4.1 %collective-permute-start.1 = (f32[32,3,256]{2,0,1:T(8,128)S(1)}, f32[32,3,256]{2,0,1:T(8,128)S(1)}, u32[]{:S(2)}, u32[]{:S(2)}) collective-permute-start(f32[32,3,256]{2,0,1:T(8,128)S(1)} %get-tuple-element.118), channel_id=1, source_target_pairs={{1,0},{2,1},{3,2},{4,3},{5,4},{6,5},{7,6},{0,7},{9,8},{10,9},{11,1... | collective-permute-start | bytes 294920 | tf_op jit(solution)/shard_map/ppermute | solution.py:21
  7.1 1.5 collective-permute-done
  9.4 12.6 %fusion.61 = f32[32,6,256]{2,0,1:T(8,128)S(1)} fusion(f32[32,6,256]{2,0,1:T(8,128)S(1)} %broadcast_select_fusion.4, f32[32,6,7,256]{3,0,2,1:T(8,128)S(1)} %bitcast.150, f32[1,6,7,256,256]{4,3,2,1,0:T(8,128)} %param.24), kind=kOutput, calls=%fused_computation.44 | convolution fusion | flops 1057013760 | bytes 12779520 | tf_op jit(solution)/shard_map/cekI,ekJI->ceJ/dot_general | solution.py:45
  22.9 2.8 %collective-permute-start.3 = (f32[32,3,256]{2,0,1:T(8,128)S(1)}, f32[32,3,256]{2,0,1:T(8,128)S(1)}, u32[]{:S(2)}, u32[]{:S(2)}) collective-permute-start(f32[32,3,256]{2,0,1:T(8,128)S(1)} %get-tuple-element.116), channel_id=1, source_target_pairs={{1,0},{2,1},{3,2},{4,3},{5,4},{6,5},{7,6},{0,7},{9,8},{10,9},{11,1... | collective-permute-start | bytes 294920 | tf_op jit(solution)/shard_map/ppermute | solution.py:21
  25.7 2.5 collective-permute-done.2
  29.1 12.7 %fusion.58 = f32[32,6,256]{2,0,1:T(8,128)S(1)} fusion(f32[32,6,256]{2,0,1:T(8,128)S(1)} %fusion.61, f32[32,6,7,256]{3,0,2,1:T(8,128)S(1)} %bitcast.151, f32[1,6,7,256,256]{4,3,2,1,0:T(8,128)} %param.24), kind=kOutput, calls=%fused_computation.43 | convolution fusion | flops 1057013760 | bytes 12779520 | tf_op jit(solution)/shard_map/cekI,ekJI->ceJ/dot_general | solution.py:45
  41.8 3.2 %collective-permute-start.4 = (f32[32,6,256]{2,0,1:T(8,128)S(1)}, f32[32,6,256]{2,0,1:T(8,128)S(1)}, u32[]{:S(2)}, u32[]{:S(2)}) collective-permute-start(f32[32,6,256]{2,0,1:T(8,128)S(1)} %fusion.58), channel_id=1, source_target_pairs={{0,16},{1,17},{2,18},{3,19},{4,20},{5,21},{6,22},{7,23},{8,24},{9,... | collective-permute-start | bytes 589832 | tf_op jit(solution)/shard_map/ppermute | solution.py:35
  45.0 4.0 %collective-permute-done.4 = f32[32,6,256]{2,0,1:T(8,128)S(1)} collective-permute-done((f32[32,6,256]{2,0,1:T(8,128)S(1)}, f32[32,6,256]{2,0,1:T(8,128)S(1)}, u32[]{:S(2)}, u32[]{:S(2)}) %collective-permute-start.4) | collective-permute-done | bytes 196640 | tf_op jit(solution)/shard_map/ppermute | solution.py:35
  49.1 3.8 %collective-permute-start.6 = (f32[32,3,256]{2,0,1:T(8,128)S(1)}, f32[32,3,256]{2,0,1:T(8,128)S(1)}, u32[]{:S(2)}, u32[]{:S(2)}) collective-permute-start(f32[32,3,256]{2,0,1:T(8,128)S(1)} %get-tuple-element.114), channel_id=1, source_target_pairs={{1,0},{2,1},{3,2},{4,3},{5,4},{6,5},{7,6},{0,7},{9,8},{10,9},{11,1... | collective-permute-start | bytes 294920 | tf_op jit(solution)/shard_map/ppermute | solution.py:21
  52.9 2.1 collective-permute-done.5
  56.0 12.6 %fusion.55 = f32[32,6,256]{2,0,1:T(8,128)S(1)} fusion(f32[32,6,256]{2,0,1:T(8,128)S(1)} %broadcast_select_fusion.5, f32[32,6,7,256]{3,0,2,1:T(8,128)S(1)} %bitcast.152, f32[1,6,7,256,256]{4,3,2,1,0:T(8,128)} %param.24), kind=kOutput, calls=%fused_computation.42 | convolution fusion | flops 1057013760 | bytes 12779520 | tf_op jit(solution)/shard_map/cekI,ekJI->ceJ/dot_general | solution.py:45
  68.7 3.7 %collective-permute-start.8 = (f32[32,3,256]{2,0,1:T(8,128)S(1)}, f32[32,3,256]{2,0,1:T(8,128)S(1)}, u32[]{:S(2)}, u32[]{:S(2)}) collective-permute-start(f32[32,3,256]{2,0,1:T(8,128)S(1)} %get-tuple-element.112), channel_id=1, source_target_pairs={{1,0},{2,1},{3,2},{4,3},{5,4},{6,5},{7,6},{0,7},{9,8},{10,9},{11,1... | collective-permute-start | bytes 294920 | tf_op jit(solution)/shard_map/ppermute | solution.py:21
  72.4 2.6 %collective-permute-done.7 = f32[32,3,256]{2,0,1:T(8,128)S(1)} collective-permute-done((f32[32,3,256]{2,0,1:T(8,128)S(1)}, f32[32,3,256]{2,0,1:T(8,128)S(1)}, u32[]{:S(2)}, u32[]{:S(2)}) %collective-permute-start.7) | collective-permute-done | bytes 98336 | tf_op jit(solution)/shard_map/ppermute | solution.py:20
  75.8 12.6 %fusion.64 = f32[32,6,256]{2,0,1:T(8,128)S(1)} fusion(f32[32,6,256]{2,0,1:T(8,128)S(1)} %fusion.58, f32[32,6,256]{2,0,1:T(8,128)S(1)} %fusion.55, f32[32,6,7,256]{3,0,2,1:T(8,128)S(1)} %bitcast.149, f32[1,6,7,256,256]{4,3,2,1,0:T(8,128)} %param.24, pred[]{:T(512)S(6)} %eq.16), kind=kOutput, calls=%fused_computation.45 | convolution fusion | flops 1057062912 | bytes 12976129 | tf_op jit(solution)/shard_map/cekI,ekJI->ceJ/dot_general | solution.py:45
  89.5 3.1 %fusion.16 = f32[64,1,32]{2,1,0:T(1,128)S(1)} fusion(f32[32,64,256]{2,1,0:T(8,128)S(1)} %convolution_bitcast_fusion, f32[64,256,1]{1,0,2:T(8,128)S(1)} %bitcast.153), kind=kOutput, calls=%fused_computation.20 | convolution fusion | flops 6291456 | bytes 2170880 | tf_op jit(solution)/shard_map/csI,sI->cs/dot_general | solution.py:68
  93.6 17.5 %fusion.6 = f32[6,32,7,256]{3,1,2,0:T(8,128)S(1)} fusion(f32[1,6,7,256,256]{4,3,2,1,0:T(8,128)} %param.24, f32[32,6,256,1]{2,1,0,3:T(8,128)S(1)} %bitcast.144), kind=kOutput, calls=%fused_computation.10 | convolution fusion | flops 1056964608 | bytes 12582912 | tf_op jit(solution)/shard_map/ceJ,ekJI->cekI/dot_general | solution.py:52
  112.7 3.6 %collective-permute-start.10 = (f32[32,3,256]{2,1,0:T(4,128)S(1)}, f32[32,3,256]{2,1,0:T(4,128)S(1)}, u32[]{:S(2)}, u32[]{:S(2)}) collective-permute-start(f32[32,3,256]{2,1,0:T(4,128)S(1)} %get-tuple-element.109), channel_id=1, source_target_pairs={{0,7},{1,0},{2,1},{3,2},{4,3},{5,4},{6,5},{7,6},{8,15},{9,8},{10,9... | collective-permute-start | bytes 294920 | tf_op jit(solution)/shard_map/ppermute | solution.py:29
  116.2 3.5 %collective-permute-done.9 = f32[32,3,256]{2,1,0:T(4,128)S(1)} collective-permute-done((f32[32,3,256]{2,1,0:T(4,128)S(1)}, f32[32,3,256]{2,1,0:T(4,128)S(1)}, u32[]{:S(2)}, u32[]{:S(2)}) %collective-permute-start.9) | collective-permute-done | bytes 98336 | tf_op jit(solution)/shard_map/ppermute | solution.py:29
  120.5 9.0 %fusion.4 = f32[6,32,7,256]{3,1,2,0:T(8,128)S(1)} fusion(f32[1,6,7,256,256]{4,3,2,1,0:T(8,128)} %param.24, f32[32,6,256,1]{2,1,0,3:T(8,128)S(1)} %fusion.77), kind=kOutput, calls=%fused_computation.8 | convolution fusion | flops 1056964608 | bytes 12582912 | tf_op jit(solution)/shard_map/ceJ,ekJI->cekI/dot_general | solution.py:52
  131.1 3.6 %collective-permute-start.12 = (f32[32,3,256]{2,1,0:T(4,128)S(1)}, f32[32,3,256]{2,1,0:T(4,128)S(1)}, u32[]{:S(2)}, u32[]{:S(2)}) collective-permute-start(f32[32,3,256]{2,1,0:T(4,128)S(1)} %get-tuple-element.107), channel_id=1, source_target_pairs={{0,7},{1,0},{2,1},{3,2},{4,3},{5,4},{6,5},{7,6},{8,15},{9,8},{10,9... | collective-permute-start | bytes 294920 | tf_op jit(solution)/shard_map/ppermute | solution.py:29
  134.6 3.5 %collective-permute-done.11 = f32[32,3,256]{2,1,0:T(4,128)S(1)} collective-permute-done((f32[32,3,256]{2,1,0:T(4,128)S(1)}, f32[32,3,256]{2,1,0:T(4,128)S(1)}, u32[]{:S(2)}, u32[]{:S(2)}) %collective-permute-start.11) | collective-permute-done | bytes 98336 | tf_op jit(solution)/shard_map/ppermute | solution.py:29
  140.3 7.0 %collective-permute-done.13 = f32[32,6,256]{2,1,0:T(8,128)S(1)} collective-permute-done((f32[32,6,256]{2,1,0:T(8,128)S(1)}, f32[32,6,256]{2,1,0:T(8,128)S(1)}, u32[]{:S(2)}, u32[]{:S(2)}) %collective-permute-start.13) | collective-permute-done | bytes 196640 | tf_op jit(solution)/shard_map/ppermute | solution.py:35
  147.3 9.0 %fusion.2 = f32[6,32,7,256]{3,1,2,0:T(8,128)S(1)} fusion(f32[1,6,7,256,256]{4,3,2,1,0:T(8,128)} %param.24, f32[32,6,256,1]{2,1,0,3:T(8,128)S(1)} %fusion.75), kind=kOutput, calls=%fused_computation.6 | convolution fusion | flops 1056964608 | bytes 12582912 | tf_op jit(solution)/shard_map/ceJ,ekJI->cekI/dot_general | solution.py:52
  156.3 1.4 fusion.34
  157.8 3.6 %collective-permute-start.15 = (f32[32,3,256]{2,1,0:T(4,128)S(1)}, f32[32,3,256]{2,1,0:T(4,128)S(1)}, u32[]{:S(2)}, u32[]{:S(2)}) collective-permute-start(f32[32,3,256]{2,1,0:T(4,128)S(1)} %get-tuple-element.105), channel_id=1, source_target_pairs={{0,7},{1,0},{2,1},{3,2},{4,3},{5,4},{6,5},{7,6},{8,15},{9,8},{10,9... | collective-permute-start | bytes 294920 | tf_op jit(solution)/shard_map/ppermute | solution.py:29
  161.4 2.6 %collective-permute-done.14 = f32[32,3,256]{2,1,0:T(4,128)S(1)} collective-permute-done((f32[32,3,256]{2,1,0:T(4,128)S(1)}, f32[32,3,256]{2,1,0:T(4,128)S(1)}, u32[]{:S(2)}, u32[]{:S(2)}) %collective-permute-start.14) | collective-permute-done | bytes 98336 | tf_op jit(solution)/shard_map/ppermute | solution.py:29
  165.0 9.0 %fusion = f32[6,32,7,256]{3,1,2,0:T(8,128)S(1)} fusion(f32[1,6,7,256,256]{4,3,2,1,0:T(8,128)} %param.24, f32[32,6,256,1]{2,1,0,3:T(8,128)S(1)} %fusion.94), kind=kOutput, calls=%fused_computation.4 | convolution fusion | flops 1056964608 | bytes 12582912 | tf_op jit(solution)/shard_map/ceJ,ekJI->cekI/dot_general | solution.py:52
  175.6 3.6 %collective-permute-start.17 = (f32[32,3,256]{2,1,0:T(4,128)S(1)}, f32[32,3,256]{2,1,0:T(4,128)S(1)}, u32[]{:S(2)}, u32[]{:S(2)}) collective-permute-start(f32[32,3,256]{2,1,0:T(4,128)S(1)} %get-tuple-element.103), channel_id=1, source_target_pairs={{0,7},{1,0},{2,1},{3,2},{4,3},{5,4},{6,5},{7,6},{8,15},{9,8},{10,9... | collective-permute-start | bytes 294920 | tf_op jit(solution)/shard_map/ppermute | solution.py:29
  179.1 3.7 %collective-permute-done.16 = f32[32,3,256]{2,1,0:T(4,128)S(1)} collective-permute-done((f32[32,3,256]{2,1,0:T(4,128)S(1)}, f32[32,3,256]{2,1,0:T(4,128)S(1)}, u32[]{:S(2)}, u32[]{:S(2)}) %collective-permute-start.16) | collective-permute-done | bytes 98336 | tf_op jit(solution)/shard_map/ppermute | solution.py:29
  183.7 1.8 collective-permute-start.18
  185.5 5.3 %all_gather.3 = f32[64,6,128]{2,0,1:T(8,128)S(1)} all-gather(f32[32,6,128]{2,0,1:T(8,128)S(1)} %constant_dynamic-slice_fusion), channel_id=1, replica_groups=mesh['sec'=2,'col'=2,'elem'=8] {'col'}, dimensions={0}, use_global_device_ids=true | all-gather | bytes 294912 | tf_op jit(solution)/shard_map/all_gather | solution.py:116
  191.2 57.6 %psum.7 = f32[32,64]{1,0:T(8,128)S(1)} all-reduce(f32[32,64]{1,0:T(8,128)S(1)} %convolution_bitcast_fusion.1), channel_id=1, replica_groups=mesh['sec'=2,'col'=2,'elem'=8] {'sec','elem'}, use_global_device_ids=true, to_apply=%region_0.2 | all-reduce | flops 2048 | bytes 16384 | tf_op jit(solution)/shard_map/psum | solution.py:121
  (91 shorter events, 19.1 us)
Async XLA Ops:
  1.6 6.9 %collective-permute-start = (f32[32,3,256]{2,0,1:T(8,128)S(1)}, f32[32,3,256]{2,0,1:T(8,128)S(1)}, u32[]{:S(2)}, u32[]{:S(2)}) collective-permute-start(f32[32,3,256]{2,0,1:T(8,128)S(1)} %get-tuple-element.117), channel_id=1, source_target_pairs={{0,1},{1,2},{2,3},{3,4},{4,5},{5,6},{6,7},{7,0},{8,9},{9,10},{10,1... | collective-permute-start | bytes 294920 | tf_op jit(solution)/shard_map/ppermute | solution.py:20
  2.2 6.4 %collective-permute-start.1 = (f32[32,3,256]{2,0,1:T(8,128)S(1)}, f32[32,3,256]{2,0,1:T(8,128)S(1)}, u32[]{:S(2)}, u32[]{:S(2)}) collective-permute-start(f32[32,3,256]{2,0,1:T(8,128)S(1)} %get-tuple-element.118), channel_id=1, source_target_pairs={{1,0},{2,1},{3,2},{4,3},{5,4},{6,5},{7,6},{0,7},{9,8},{10,9},{11,1... | collective-permute-start | bytes 294920 | tf_op jit(solution)/shard_map/ppermute | solution.py:21
  22.0 6.2 %collective-permute-start.2 = (f32[32,3,256]{2,0,1:T(8,128)S(1)}, f32[32,3,256]{2,0,1:T(8,128)S(1)}, u32[]{:S(2)}, u32[]{:S(2)}) collective-permute-start(f32[32,3,256]{2,0,1:T(8,128)S(1)} %get-tuple-element.115), channel_id=1, source_target_pairs={{0,1},{1,2},{2,3},{3,4},{4,5},{5,6},{6,7},{7,0},{8,9},{9,10},{10,1... | collective-permute-start | bytes 294920 | tf_op jit(solution)/shard_map/ppermute | solution.py:20
  22.9 5.3 %collective-permute-start.3 = (f32[32,3,256]{2,0,1:T(8,128)S(1)}, f32[32,3,256]{2,0,1:T(8,128)S(1)}, u32[]{:S(2)}, u32[]{:S(2)}) collective-permute-start(f32[32,3,256]{2,0,1:T(8,128)S(1)} %get-tuple-element.116), channel_id=1, source_target_pairs={{1,0},{2,1},{3,2},{4,3},{5,4},{6,5},{7,6},{0,7},{9,8},{10,9},{11,1... | collective-permute-start | bytes 294920 | tf_op jit(solution)/shard_map/ppermute | solution.py:21
  29.1 19.9 %copy-start = (f32[32,6,256]{2,0,1:T(8,128)S(1)}, f32[32,6,256]{2,0,1:T(8,128)}, u32[]{:S(2)}) copy-start(f32[32,6,256]{2,0,1:T(8,128)} %param.23) | copy-start | bytes 589828
  41.8 7.2 %collective-permute-start.4 = (f32[32,6,256]{2,0,1:T(8,128)S(1)}, f32[32,6,256]{2,0,1:T(8,128)S(1)}, u32[]{:S(2)}, u32[]{:S(2)}) collective-permute-start(f32[32,6,256]{2,0,1:T(8,128)S(1)} %fusion.58), channel_id=1, source_target_pairs={{0,16},{1,17},{2,18},{3,19},{4,20},{5,21},{6,22},{7,23},{8,24},{9,... | collective-permute-start | bytes 589832 | tf_op jit(solution)/shard_map/ppermute | solution.py:35
  49.1 5.9 %collective-permute-start.5 = (f32[32,3,256]{2,0,1:T(8,128)S(1)}, f32[32,3,256]{2,0,1:T(8,128)S(1)}, u32[]{:S(2)}, u32[]{:S(2)}) collective-permute-start(f32[32,3,256]{2,0,1:T(8,128)S(1)} %get-tuple-element.113), channel_id=1, source_target_pairs={{0,1},{1,2},{2,3},{3,4},{4,5},{5,6},{6,7},{7,0},{8,9},{9,10},{10,1... | collective-permute-start | bytes 294920 | tf_op jit(solution)/shard_map/ppermute | solution.py:20
  49.1 6.0 %collective-permute-start.6 = (f32[32,3,256]{2,0,1:T(8,128)S(1)}, f32[32,3,256]{2,0,1:T(8,128)S(1)}, u32[]{:S(2)}, u32[]{:S(2)}) collective-permute-start(f32[32,3,256]{2,0,1:T(8,128)S(1)} %get-tuple-element.114), channel_id=1, source_target_pairs={{1,0},{2,1},{3,2},{4,3},{5,4},{6,5},{7,6},{0,7},{9,8},{10,9},{11,1... | collective-permute-start | bytes 294920 | tf_op jit(solution)/shard_map/ppermute | solution.py:21
  55.9 16.4 %copy-start.3 = (s32[64]{0:T(128)S(1)}, s32[64]{0:T(128)}, u32[]{:S(2)}) copy-start(s32[64]{0:T(128)} %param.26) | copy-start | bytes 772
  68.6 6.3 %collective-permute-start.7 = (f32[32,3,256]{2,0,1:T(8,128)S(1)}, f32[32,3,256]{2,0,1:T(8,128)S(1)}, u32[]{:S(2)}, u32[]{:S(2)}) collective-permute-start(f32[32,3,256]{2,0,1:T(8,128)S(1)} %get-tuple-element.111), channel_id=1, source_target_pairs={{0,1},{1,2},{2,3},{3,4},{4,5},{5,6},{6,7},{7,0},{8,9},{9,10},{10,1... | collective-permute-start | bytes 294920 | tf_op jit(solution)/shard_map/ppermute | solution.py:20
  68.7 6.3 %collective-permute-start.8 = (f32[32,3,256]{2,0,1:T(8,128)S(1)}, f32[32,3,256]{2,0,1:T(8,128)S(1)}, u32[]{:S(2)}, u32[]{:S(2)}) collective-permute-start(f32[32,3,256]{2,0,1:T(8,128)S(1)} %get-tuple-element.112), channel_id=1, source_target_pairs={{1,0},{2,1},{3,2},{4,3},{5,4},{6,5},{7,6},{0,7},{9,8},{10,9},{11,1... | collective-permute-start | bytes 294920 | tf_op jit(solution)/shard_map/ppermute | solution.py:21
  88.5 1.0 copy-start.2
  112.6 7.2 %collective-permute-start.9 = (f32[32,3,256]{2,1,0:T(4,128)S(1)}, f32[32,3,256]{2,1,0:T(4,128)S(1)}, u32[]{:S(2)}, u32[]{:S(2)}) collective-permute-start(f32[32,3,256]{2,1,0:T(4,128)S(1)} %get-tuple-element.110), channel_id=1, source_target_pairs={{0,1},{1,2},{2,3},{3,4},{4,5},{5,6},{6,7},{7,0},{8,9},{9,10},{10,1... | collective-permute-start | bytes 294920 | tf_op jit(solution)/shard_map/ppermute | solution.py:29
  112.7 7.4 %collective-permute-start.10 = (f32[32,3,256]{2,1,0:T(4,128)S(1)}, f32[32,3,256]{2,1,0:T(4,128)S(1)}, u32[]{:S(2)}, u32[]{:S(2)}) collective-permute-start(f32[32,3,256]{2,1,0:T(4,128)S(1)} %get-tuple-element.109), channel_id=1, source_target_pairs={{0,7},{1,0},{2,1},{3,2},{4,3},{5,4},{6,5},{7,6},{8,15},{9,8},{10,9... | collective-permute-start | bytes 294920 | tf_op jit(solution)/shard_map/ppermute | solution.py:29
  131.0 7.2 %collective-permute-start.11 = (f32[32,3,256]{2,1,0:T(4,128)S(1)}, f32[32,3,256]{2,1,0:T(4,128)S(1)}, u32[]{:S(2)}, u32[]{:S(2)}) collective-permute-start(f32[32,3,256]{2,1,0:T(4,128)S(1)} %get-tuple-element.108), channel_id=1, source_target_pairs={{0,1},{1,2},{2,3},{3,4},{4,5},{5,6},{6,7},{7,0},{8,9},{9,10},{10,1... | collective-permute-start | bytes 294920 | tf_op jit(solution)/shard_map/ppermute | solution.py:29
  131.1 7.5 %collective-permute-start.12 = (f32[32,3,256]{2,1,0:T(4,128)S(1)}, f32[32,3,256]{2,1,0:T(4,128)S(1)}, u32[]{:S(2)}, u32[]{:S(2)}) collective-permute-start(f32[32,3,256]{2,1,0:T(4,128)S(1)} %get-tuple-element.107), channel_id=1, source_target_pairs={{0,7},{1,0},{2,1},{3,2},{4,3},{5,4},{6,5},{7,6},{8,15},{9,8},{10,9... | collective-permute-start | bytes 294920 | tf_op jit(solution)/shard_map/ppermute | solution.py:29
  139.0 8.3 %collective-permute-start.13 = (f32[32,6,256]{2,1,0:T(8,128)S(1)}, f32[32,6,256]{2,1,0:T(8,128)S(1)}, u32[]{:S(2)}, u32[]{:S(2)}) collective-permute-start(f32[32,6,256]{2,1,0:T(8,128)S(1)} %fusion.76), channel_id=1, source_target_pairs={{16,0},{17,1},{18,2},{19,3},{20,4},{21,5},{22,6},{23,7},{24,8},{25... | collective-permute-start | bytes 589832 | tf_op jit(solution)/shard_map/ppermute | solution.py:35
  157.7 6.2 %collective-permute-start.14 = (f32[32,3,256]{2,1,0:T(4,128)S(1)}, f32[32,3,256]{2,1,0:T(4,128)S(1)}, u32[]{:S(2)}, u32[]{:S(2)}) collective-permute-start(f32[32,3,256]{2,1,0:T(4,128)S(1)} %get-tuple-element.106), channel_id=1, source_target_pairs={{0,1},{1,2},{2,3},{3,4},{4,5},{5,6},{6,7},{7,0},{8,9},{9,10},{10,1... | collective-permute-start | bytes 294920 | tf_op jit(solution)/shard_map/ppermute | solution.py:29
  157.8 6.7 %collective-permute-start.15 = (f32[32,3,256]{2,1,0:T(4,128)S(1)}, f32[32,3,256]{2,1,0:T(4,128)S(1)}, u32[]{:S(2)}, u32[]{:S(2)}) collective-permute-start(f32[32,3,256]{2,1,0:T(4,128)S(1)} %get-tuple-element.105), channel_id=1, source_target_pairs={{0,7},{1,0},{2,1},{3,2},{4,3},{5,4},{6,5},{7,6},{8,15},{9,8},{10,9... | collective-permute-start | bytes 294920 | tf_op jit(solution)/shard_map/ppermute | solution.py:29
  175.4 7.4 %collective-permute-start.16 = (f32[32,3,256]{2,1,0:T(4,128)S(1)}, f32[32,3,256]{2,1,0:T(4,128)S(1)}, u32[]{:S(2)}, u32[]{:S(2)}) collective-permute-start(f32[32,3,256]{2,1,0:T(4,128)S(1)} %get-tuple-element.104), channel_id=1, source_target_pairs={{0,1},{1,2},{2,3},{3,4},{4,5},{5,6},{6,7},{7,0},{8,9},{9,10},{10,1... | collective-permute-start | bytes 294920 | tf_op jit(solution)/shard_map/ppermute | solution.py:29
  175.6 7.6 %collective-permute-start.17 = (f32[32,3,256]{2,1,0:T(4,128)S(1)}, f32[32,3,256]{2,1,0:T(4,128)S(1)}, u32[]{:S(2)}, u32[]{:S(2)}) collective-permute-start(f32[32,3,256]{2,1,0:T(4,128)S(1)} %get-tuple-element.103), channel_id=1, source_target_pairs={{0,7},{1,0},{2,1},{3,2},{4,3},{5,4},{6,5},{7,6},{8,15},{9,8},{10,9... | collective-permute-start | bytes 294920 | tf_op jit(solution)/shard_map/ppermute | solution.py:29
  183.7 7.1 %collective-permute-start.18 = (f32[32,6,128]{2,1,0:T(8,128)S(1)}, f32[32,6,128]{2,1,0:T(8,128)S(1)}, u32[]{:S(2)}, u32[]{:S(2)}) collective-permute-start(f32[32,6,128]{2,1,0:T(8,128)S(1)} %slice.329), channel_id=1, source_target_pairs={{0,16},{1,17},{2,18},{3,19},{4,20},{5,21},{6,22},{7,23},{8,24},{9,... | collective-permute-start | bytes 294920 | tf_op jit(solution)/shard_map/ppermute | solution.py:35
  190.9 58.5 %copy-start.1 = (f32[32,6,128]{2,0,1:T(8,128)}, f32[32,6,128]{2,0,1:T(8,128)S(1)}, u32[]{:S(2)}) copy-start(f32[32,6,128]{2,0,1:T(8,128)S(1)} %copy.26) | copy-start | bytes 294916
where the time goes:
time: 252 us; the launch traced here: 250 us
  matrix products  106 us (42%)
  blocking collectives  62.9 us (25%)
  starting transfers between devices  36.8 us (15%)
  waiting for transfers between devices  33 us (13%)
  local copies, waits for them, and re-layouts  5.85 us (2%)
  other arithmetic  3.7 us (1%)
    psum x1, blocking collectives, per_device(): gram = lax.psum(partial_gram, ('sec', 'elem')) * scaling  57.6 us
    dot_general x4, matrix products, tangent_pass(): jnp.einsum('cekI,ekJI->ceJ', gathered, blocks, precision=PRECISE)  50.6 us
    dot_general x4, matrix products, adjoint_pass(): products = jnp.einsum('ceJ,ekJI->cekI', vector, blocks, precision=PRECISE)  44.5 us
    ppermute x8, starting transfers between devices, from_behind(): return lax.ppermute(value, axis, pairs)  14.5 us
    ppermute x4, starting transfers between devices, with_halo(): after = lax.ppermute(leading, axis, down)  14.3 us
    ppermute x8, waiting for transfers between devices, from_behind(): return lax.ppermute(value, axis, pairs)  13.3 us
    ppermute x3, waiting for transfers between devices, from_behind_2(): lax.ppermute(value, axis, [(source, source + steps) for source in range(l...  11 us
    ppermute x4, waiting for transfers between devices, with_halo(): before = lax.ppermute(last, axis, up)  8.62 us
  transfers between devices with their start and end apart: 19, of which 11 were waited for; matrix products, arithmetic and copies ran while one was open for 1% of the time, Pallas kernels for 0%

commit v1 on v0

v1 whole, which is shorter than its diff:
```python
import functools
import math

import jax
import jax.numpy as jnp
from jax import lax
from jax.experimental import pallas as pl
from jax.experimental.pallas import tpu as pltpu
from jax.sharding import PartitionSpec as P

STEPS = 2
MESH = pl.DeviceIdType.MESH
F32 = jnp.float32
BF16 = jnp.bfloat16
LANES = 128


def halves(value):
    high = value.astype(BF16)
    low = (value - high.astype(F32)).astype(BF16)
    return high, low


def product(a, b, transposed):
    dims = (((1,), (1 if transposed else 0,)), ((), ()))
    return lax.dot_general(a, b, dims, preferred_element_type=F32)


def product3(stack, high, low, transposed):
    rows = stack.shape[0] // 2
    first = product(stack, high, transposed)
    second = product(stack[:rows], low, transposed)
    return first[:rows] + (first[rows:] + second)


def kernel(
    sizes,
    neighbors,
    stations,
    probes_hbm,
    jacobian_hbm,
    weights_hbm,
    hess_ref,
    gram_ref,
    *scratch,
):
    cols, elems, order, nbrs, stats, n_elem, n_col = sizes
    radius = (nbrs - 1) // 2
    width = radius * order
    half = order // 2
    jac_f32 = scratch[:elems]
    jac_high = scratch[elems : 2 * elems]
    jac_low = scratch[2 * elems : 3 * elems]
    (
        probes_ref, weights_ref, state, state_in, field, from_left, from_right,
        adjoint, adjoint_in, observed, out_left, out_right, back_left, back_right,
        readings, partial, partial_in, upper, upper_in,
        load_sem, send_sem, recv_sem,
    ) = scratch[3 * elems :]
    section = lax.axis_index("sec")
    column = lax.axis_index("col")
    block = lax.axis_index("elem")
    left = lax.rem(block + n_elem - 1, n_elem)
    right = lax.rem(block + 1, n_elem)
    first_elem = block * elems
    elem_total = elems * n_elem
    rounds = int(math.log2(n_elem))

    probe_load = pltpu.make_async_copy(probes_hbm, probes_ref, load_sem.at[elems])
    probe_load.start()
    jac_loads = [
        pltpu.make_async_copy(jacobian_hbm.at[0, e], jac_f32[e], load_sem.at[e])
        for e in range(elems)
    ]
    for load in jac_loads:
        load.start()
    weights_load = pltpu.make_async_copy(
        weights_hbm, weights_ref.at[pl.ds(0, stats)], load_sem.at[elems + 1]
    )
    weights_load.start()

    barrier = pltpu.get_barrier_semaphore()
    partners = [{"elem": left}, {"elem": right}, {"sec": 1 - section}]
    partners += [{"col": lax.rem(column + j, n_col)} for j in range(1, n_col)]
    flips = []
    for r in range(rounds):
        bit = 1 << r
        upper_bit = lax.rem(block // bit, 2)
        flips.append({"elem": block + bit - 2 * bit * upper_bit})
    for partner in partners + flips:
        pl.semaphore_signal(barrier, inc=1, device_id=partner, device_id_type=MESH)
    pl.semaphore_wait(barrier, len(partners) + len(flips))

    def remote(src, dst, index, target):
        return pltpu.make_async_remote_copy(
            src_ref=src, dst_ref=dst, send_sem=send_sem.at[index],
            recv_sem=recv_sem.at[index], device_id=target, device_id_type=MESH,
        )

    FORWARD, BACKWARD, UPPER, GRAM, READ = (4 * STEPS + i for i in range(5))
    FLIP = READ + n_col - 1

    probe_load.wait()

    @pl.when(section == 0)
    def _():
        for e in range(elems):
            state[0, :, e * order : (e + 1) * order] = probes_ref[:, e, :]

    forward = remote(state.at[STEPS], state_in, FORWARD, {"sec": 1 - section})

    def halo_copies(t):
        return (
            remote(state.at[t, :, pl.ds(0, width)], from_right.at[t], 2 * t, {"elem": left}),
            remote(
                state.at[t, :, pl.ds(elems * order - width, width)],
                from_left.at[t], 2 * t + 1, {"elem": right},
            ),
        )

    @pl.when(section == 0)
    def _():
        for copy in halo_copies(0):
            copy.start()

    for e in range(elems):
        jac_loads[e].wait()

        def split_one(d, carry, e=e):
            target = lax.rem(first_elem + e + d - radius + elem_total, elem_total)
            slot = jnp.int32(0)
            for k in range(1, nbrs):
                slot = jnp.where(neighbors[e, k] == target, jnp.int32(k), slot)
            high, low = halves(jac_f32[e][slot])
            lanes = pl.ds(pl.multiple_of(d * order, order), order)
            jac_high[e][:, lanes] = high
            jac_low[e][:, lanes] = low
            return carry

        lax.fori_loop(0, nbrs, split_one, 0)

    weights_load.wait()
    weights_ref[stats:, :] = jnp.zeros((weights_ref.shape[0] - stats, order), F32)
    weights_high, weights_low = halves(weights_ref[...])
    lane_ids = lax.broadcasted_iota(jnp.int32, (cols, LANES), 1)
    station_row = jnp.full((cols, LANES), -1, jnp.int32)
    for i in range(stats):
        station_row = jnp.where(lane_ids == i, stations[i], station_row)

    @pl.when(section == 1)
    def _():
        forward.wait_recv()
        state[0] = state_in[...]
        for copy in halo_copies(0):
            copy.start()

    def put_field(start, value):
        high, low = halves(value)
        field[:cols, start : start + value.shape[1]] = high
        field[cols:, start : start + value.shape[1]] = low

    def blocks(ref, begin, end):
        return ref[:, begin * order : end * order]

    def tangent(t, carry):
        to_left, to_right = halo_copies(t)

        @pl.when(t > 0)
        def _():
            to_left.start()
            to_right.start()

        put_field(width, state[t])
        for e in range(elems):
            low, high = max(e, radius), min(e + nbrs, radius + elems)
            added = product3(
                blocks(field, low, high), blocks(jac_high[e], low - e, high - e),
                blocks(jac_low[e], low - e, high - e), True,
            )
            here = slice(e * order, (e + 1) * order)
            state[t + 1, :, here] = state[t, :, here] + added
        to_left.wait_recv()
        to_right.wait_recv()
        put_field(0, from_left[t])
        put_field(width + elems * order, from_right[t])
        for e in range(elems):
            here = slice(e * order, (e + 1) * order)
            spans = []
            if e < radius:
                spans.append((e, radius))
            if e + nbrs > radius + elems:
                spans.append((radius + elems, e + nbrs))
            total = state[t + 1, :, here]
            for low, high in spans:
                total = total + product3(
                    blocks(field, low, high), blocks(jac_high[e], low - e, high - e),
                    blocks(jac_low[e], low - e, high - e), True,
                )
            state[t + 1, :, here] = total
        to_left.wait_send()
        to_right.wait_send()
        return carry

    lax.fori_loop(0, STEPS, tangent, 0)

    @pl.when(section == 0)
    def _():
        forward.start()

    reading = jnp.zeros((cols, LANES), F32)
    for e in range(elems):
        here = slice(e * order, (e + 1) * order)
        stack = jnp.concatenate(halves(state[STEPS, :, here]), axis=0)
        read = product3(stack, weights_high, weights_low, True)
        read = jnp.where(station_row == first_elem + e, read, 0.0)
        reading = reading + read
        stack = jnp.concatenate(halves(read), axis=0)
        observed[:, here] = product3(stack, weights_high, weights_low, False)
    for slot in range(n_col, readings.shape[0]):
        readings[slot] = jnp.zeros((cols, LANES), F32)
    readings[column] = reading
    read_copies = [
        remote(
            readings.at[column], readings.at[column], READ + j - 1,
            {"col": lax.rem(column + j, n_col)},
        )
        for j in range(1, n_col)
    ]
    for copy in read_copies:
        copy.start()
    gram_copy = remote(partial.at[rounds], partial_in.at[rounds], GRAM, {"sec": 1 - section})

    def project():
        for copy in read_copies:
            copy.wait_recv()
        everyone = readings[...].reshape(readings.shape[0] * cols, LANES)
        high, low = halves(everyone)
        stack = jnp.concatenate(halves(readings[column]), axis=0)
        partial[0] = product3(stack, high, low, True)
        for r in range(rounds):
            copy = remote(partial.at[r], partial_in.at[r], FLIP + r, flips[r])
            copy.start()
            copy.wait_recv()
            partial[r + 1] = partial[r] + partial_in[r]
            copy.wait_send()
        gram_copy.start()

    backward = remote(adjoint.at[STEPS], adjoint_in, BACKWARD, {"sec": 1 - section})

    @pl.when(section == 0)
    def _():
        project()
        backward.wait_recv()
        adjoint[0] = adjoint_in[...] + observed[...]

    @pl.when(section == 1)
    def _():
        adjoint[0] = observed[...]

    def adjoint_step(t, carry):
        put_field(0, adjoint[t])
        parts = [field[:, e * order : (e + 1) * order] for e in range(elems)]

        def term(e, low, high):
            return product3(
                parts[e], blocks(jac_high[e], low - e, high - e),
                blocks(jac_low[e], low - e, high - e), False,
            )

        out_left[t] = term(0, 0, radius)
        for e in range(1, radius):
            out_left[t, :, e * order : width] = out_left[t, :, e * order : width] + term(e, e, radius)
        edge = radius + elems
        out_right[t] = term(elems - 1, edge, edge + radius)
        for e in range(elems - radius, elems - 1):
            size = (e + nbrs - edge) * order
            out_right[t, :, :size] = out_right[t, :, :size] + term(e, edge, e + nbrs)
        to_left = remote(out_left.at[t], back_right.at[t], 2 * STEPS + 2 * t, {"elem": left})
        to_right = remote(out_right.at[t], back_left.at[t], 2 * STEPS + 2 * t + 1, {"elem": right})
        to_left.start()
        to_right.start()
        adjoint[t + 1] = adjoint[t]
        for e in range(elems):
            low, high = max(e, radius), min(e + nbrs, edge)
            here = slice((low - radius) * order, (high - radius) * order)
            adjoint[t + 1, :, here] = adjoint[t + 1, :, here] + term(e, low, high)
        to_left.wait_recv()
        to_right.wait_recv()
        adjoint[t + 1, :, :width] = adjoint[t + 1, :, :width] + back_left[t]
        tail = slice(elems * order - width, elems * order)
        adjoint[t + 1, :, tail] = adjoint[t + 1, :, tail] + back_right[t]
        to_left.wait_send()
        to_right.wait_send()
        return carry

    lax.fori_loop(0, STEPS, adjoint_step, 0)

    up = remote(upper, upper_in, UPPER, {"sec": 1 - section})

    @pl.when(section == 0)
    def _():
        for e in range(elems):
            upper[e] = adjoint[STEPS, :, e * order + half : (e + 1) * order]
        up.start()
        for e in range(elems):
            hess_ref[e] = adjoint[STEPS, :, e * order : e * order + half]

    @pl.when(section == 1)
    def _():
        backward.start()
        project()

    gram_copy.wait_recv()
    scale = 1.0 / (elem_total * order)
    gram_ref[...] = (partial[rounds] + partial_in[rounds]) * scale

    @pl.when(section == 0)
    def _():
        up.wait_send()
        forward.wait_send()

    @pl.when(section == 1)
    def _():
        up.wait_recv()
        hess_ref[...] = upper_in[...]
        backward.wait_send()

    gram_copy.wait_send()
    for copy in read_copies:
        copy.wait_send()


def per_device(n_elem, n_col, probes, jacobian, neighbors, stations, obs_weights):
    cols, elems, order = probes.shape
    nbrs = neighbors.shape[1]
    stats = stations.shape[0]
    radius = (nbrs - 1) // 2
    rounds = int(math.log2(n_elem))
    slots = max(n_col, LANES // cols)
    sizes = (cols, elems, order, nbrs, stats, n_elem, n_col)
    full, width = elems * order, radius * order
    copies = 4 * STEPS + 4 + (n_col - 1) + rounds
    scratch = [pltpu.VMEM((nbrs, order, order), F32)] * elems
    scratch += [pltpu.VMEM((order, nbrs * order), BF16)] * (2 * elems)
    scratch += [
        pltpu.VMEM((cols, elems, order), F32),
        pltpu.VMEM((LANES, order), F32),
        pltpu.VMEM((STEPS + 1, cols, full), F32),
        pltpu.VMEM((cols, full), F32),
        pltpu.VMEM((2 * cols, full + 2 * width), BF16),
        pltpu.VMEM((STEPS, cols, width), F32),
        pltpu.VMEM((STEPS, cols, width), F32),
        pltpu.VMEM((STEPS + 1, cols, full), F32),
        pltpu.VMEM((cols, full), F32),
        pltpu.VMEM((cols, full), F32),
        pltpu.VMEM((STEPS, cols, width), F32),
        pltpu.VMEM((STEPS, cols, width), F32),
        pltpu.VMEM((STEPS, cols, width), F32),
        pltpu.VMEM((STEPS, cols, width), F32),
        pltpu.VMEM((slots, cols, LANES), F32),
        pltpu.VMEM((rounds + 1, cols, slots * cols), F32),
        pltpu.VMEM((rounds + 1, cols, slots * cols), F32),
        pltpu.VMEM((elems, cols, order // 2), F32),
        pltpu.VMEM((elems, cols, order // 2), F32),
        pltpu.SemaphoreType.DMA((elems + 2,)),
        pltpu.SemaphoreType.DMA((copies,)),
        pltpu.SemaphoreType.DMA((copies,)),
    ]
    smem = pl.BlockSpec(memory_space=pltpu.SMEM)
    anywhere = pl.BlockSpec(memory_space=pl.ANY)
    vmem = pl.BlockSpec(memory_space=pltpu.VMEM)
    hess, gram = pl.pallas_call(
        functools.partial(kernel, sizes),
        out_shape=(
            jax.ShapeDtypeStruct((elems, cols, order // 2), F32),
            jax.ShapeDtypeStruct((cols, slots * cols), F32),
        ),
        in_specs=[smem, smem, anywhere, anywhere, anywhere],
        out_specs=(vmem, vmem),
        scratch_shapes=scratch,
        compiler_params=pltpu.CompilerParams(
            collective_id=0, has_side_effects=True, vmem_limit_bytes=56 * 1024 * 1024
        ),
    )(neighbors, stations, probes, jacobian, obs_weights)
    return hess.transpose(1, 0, 2), gram[:, : n_col * cols]


def solution(mesh):
    in_specs = (
        P("col", "elem", None),
        P("sec", "elem", None, None, None),
        P("elem", None),
        P("elem"),
        P("elem", None),
    )
    out_specs = (P("col", "elem", "sec"), P("col", None))
    body = functools.partial(per_device, mesh.shape["elem"], mesh.shape["col"])
    return jax.shard_map(
        body, mesh=mesh, in_specs=in_specs, out_specs=out_specs, check_vma=False
    )
```

time: 252 us -> 68.9 us (0.27)
  matrix products: 106 us -> 0 us
  Pallas kernels: 0 us -> 63.3 us
  blocking collectives: 62.9 us -> 0 us
  starting transfers between devices: 36.8 us -> 0 us
  waiting for transfers between devices: 33 us -> 0 us
  other arithmetic: 3.7 us -> 0 us
    dot_general x16 -> x0, matrix products: 106 us -> none  [the longest x4 50.6 us: tangent_pass(): jnp.einsum('cekI,ekJI->ceJ', gathered, blocks, precision=PRECISE)]
    pallas_call x0 -> x1, Pallas kernels: none -> 63.3 us  [per_device(): pl.pallas_call(functools.partial(kernel, sizes), out_shape=(jax.ShapeDtyp...]
    psum x1 -> x0, blocking collectives: 57.6 us -> none  [per_device(): gram = lax.psum(partial_gram, ('sec', 'elem')) * scaling]
    ppermute x19 -> x0, starting transfers between devices: 36.8 us -> none  [the longest x8 14.5 us: from_behind(): return lax.ppermute(value, axis, pairs)]
    ppermute x19 -> x0, waiting for transfers between devices: 33 us -> none  [the longest x8 13.3 us: from_behind(): return lax.ppermute(value, axis, pairs)]
    all_gather x1 -> x0, blocking collectives: 5.29 us -> none  [per_device(): shard_piece = lax.all_gather(probe_half, 'col', axis=0, tiled=True)]
    unnamed x9 -> x3, local copies, waits for them, and re-layouts: 0.05 us -> 4.6 us
    scatter-add x8 -> x0, local copies, waits for them, and re-layouts: 2.69 us -> none  [the longest x4 1.45 us: adjoint_pass(): centre = centre.at[:, :radius].add(from_left)]
  transfers between devices with their start and end apart: 19 -> 0, of which waited for: 11 -> 0; matrix products, arithmetic and copies ran while one was open for 1% -> 0% of each run, Pallas kernels for 0% -> 0%
where the time goes in v1:
time: 68.9 us; the launch traced here: 68.5 us
  Pallas kernels  63.3 us (92%)
  local copies, waits for them, and re-layouts  4.6 us (7%)
    pallas_call x1, Pallas kernels, per_device(): pl.pallas_call(functools.partial(kernel, sizes), out_shape=(jax.ShapeDtyp...  63.3 us
    unnamed x3, local copies, waits for them, and re-layouts  4.6 us

profile of v1, /device:TPU:0, one launch (start us, length us, event | category | flops | bytes accessed | tf_op | source)
XLA Modules:
  0.0 68.5 jit_solution(4802453566494351423)
XLA Ops:
  0.6 1.7 %copy.7.probes_hbm = f32[32,6,256]{2,1,0:T(8,128)} copy(f32[32,6,256]{2,0,1:T(8,128)} %param.5) | data formatting | bytes 393216 | tf_op args[0]
  2.4 63.3 %shard_map.68 = (f32[6,32,128]{2,1,0:T(8,128)}, f32[32,128]{1,0:T(8,128)}) custom-call(s32[6,7]{1,0:T(8,128)} %neighbors.1, s32[64]{0:T(128)} %stations.1, f32[32,6,256]{2,1,0:T(8,128)} %copy.7.probes_hbm, f32[1,6,7,256,256]{4,3,2,1,0:T(8,128)} %jacobian_hbm.1, f32[64,256]{1,0:T(8,128)} %weights_hbm.1), custom_call_target="tpu_custom_call" | custom-call | tf_op jit(solution)/shard_map/pallas_call | solution.py:372
  65.7 1.5 %copy.10 = f32[32,6,128]{2,0,1:T(8,128)} copy(f32[32,6,128]{2,0,1:T(8,128)} %bitcast.2) | data formatting | bytes 196608
  67.2 1.3 %copy.11 = f32[32,64]{1,0:T(8,128)} copy(f32[32,64]{1,0:T(8,128)} %bitcast.3) | data formatting | bytes 16384

commit v2 on v1

v2 whole, which is shorter than its diff:
```python
import functools
import math

import jax
import jax.numpy as jnp
from jax import lax
from jax.experimental import pallas as pl
from jax.experimental.pallas import tpu as pltpu
from jax.sharding import PartitionSpec as P

STEPS = 2
MESH = pl.DeviceIdType.MESH
F32 = jnp.float32
BF16 = jnp.bfloat16
LANES = 128


def halves(value):
    high = value.astype(BF16)
    low = (value - high.astype(F32)).astype(BF16)
    return high, low


def product(a, b, transposed):
    dims = (((1,), (1 if transposed else 0,)), ((), ()))
    return lax.dot_general(a, b, dims, preferred_element_type=F32)


def product3(stack, high, low, transposed):
    rows = stack.shape[0] // 2
    first = product(stack, high, transposed)
    second = product(stack[:rows], low, transposed)
    return first[:rows] + (first[rows:] + second)


def kernel(
    sizes,
    neighbors,
    stations,
    probes_hbm,
    jacobian_hbm,
    weights_hbm,
    hess_ref,
    gram_ref,
    *scratch,
):
    cols, elems, order, nbrs, stats, n_elem, n_col = sizes
    radius = (nbrs - 1) // 2
    width = radius * order
    half = order // 2
    jac_f32 = scratch[:elems]
    jac_high = scratch[elems : 2 * elems]
    jac_low = scratch[2 * elems : 3 * elems]
    (
        probes_ref, weights_ref, state, field, halo_left, halo_right,
        adjoint, adjoint_in, observed, out_left, out_right, back_left, back_right,
        back_across, readings, partial, partial_in, upper, upper_in,
        load_sem, send_sem, recv_sem,
    ) = scratch[3 * elems :]
    section = lax.axis_index("sec")
    column = lax.axis_index("col")
    block = lax.axis_index("elem")
    left = lax.rem(block + n_elem - 1, n_elem)
    right = lax.rem(block + 1, n_elem)
    even = lax.rem(block, 2) == 0
    far = jnp.where(even, left, right)
    other = 1 - section
    first_elem = block * elems
    elem_total = elems * n_elem
    rounds = int(math.log2(n_elem))
    edge = radius + elems
    full = elems * order
    last = STEPS - 1
    LEFT, RIGHT = 0, 1
    neighbour = (left, right)
    halo_in = (halo_left, halo_right)
    out = (out_left, out_right)
    back = (back_left, back_right)
    own = (slice(0, width), slice(full - width, full))
    own_ds = (pl.ds(0, width), pl.ds(full - width, width))
    own_elems = (range(0, radius), range(elems - radius, elems))

    def by_parity(run):
        @pl.when(even)
        def _():
            run(RIGHT, LEFT)

        @pl.when(jnp.logical_not(even))
        def _():
            run(LEFT, RIGHT)

    probe_load = pltpu.make_async_copy(probes_hbm, probes_ref, load_sem.at[elems])
    probe_load.start()
    jac_loads = [
        pltpu.make_async_copy(jacobian_hbm.at[0, e], jac_f32[e], load_sem.at[e])
        for e in range(elems)
    ]
    for load in jac_loads:
        load.start()
    weights_load = pltpu.make_async_copy(
        weights_hbm, weights_ref.at[pl.ds(0, stats)], load_sem.at[elems + 1]
    )
    weights_load.start()

    barrier = pltpu.get_barrier_semaphore()
    partners = [{"elem": left}, {"elem": right}, {"sec": other}, {"sec": other, "elem": far}]
    partners += [{"col": lax.rem(column + j, n_col)} for j in range(1, n_col)]
    flips = []
    for r in range(rounds):
        bit = 1 << r
        upper_bit = lax.rem(block // bit, 2)
        flips.append({"elem": block + bit - 2 * bit * upper_bit})
    for partner in partners + flips:
        pl.semaphore_signal(barrier, inc=1, device_id=partner, device_id_type=MESH)

    probe_load.wait()

    @pl.when(section == 0)
    def _():
        for e in range(elems):
            state[0, :, e * order : (e + 1) * order] = probes_ref[e]

    pl.semaphore_wait(barrier, len(partners) + len(flips))

    def remote(src, dst, index, target, arrival=None):
        arrival = index if arrival is None else arrival
        return pltpu.make_async_remote_copy(
            src_ref=src, dst_ref=dst, send_sem=send_sem.at[index],
            recv_sem=recv_sem.at[arrival], device_id=target, device_id_type=MESH,
        )

    FORWARD = 4 * STEPS
    BACKWARD, UPPER = FORWARD + 2, FORWARD + 4
    ACROSS, RETURN, GRAM, READ = (FORWARD + 6 + i for i in range(4))
    FLIP = READ + n_col - 1

    def halo_copy(t, side):
        return remote(
            state.at[t, :, own_ds[side]], halo_in[1 - side].at[t], 2 * t + side,
            {"elem": neighbour[side]},
        )

    def halo_across(side):
        return remote(
            state.at[STEPS, :, own_ds[side]], halo_in[1 - side].at[0], ACROSS,
            {"sec": other, "elem": neighbour[side]}, side,
        )

    def forward(side):
        return remote(
            state.at[STEPS, :, own_ds[side]], state.at[0, :, own_ds[side]],
            FORWARD + side, {"sec": other},
        )

    def out_copy(t, side):
        return remote(
            out[side].at[t], back[1 - side].at[t], 2 * STEPS + 2 * t + side,
            {"elem": neighbour[side]},
        )

    def out_across(side):
        return remote(
            out[side].at[last], back_across, RETURN, {"sec": other, "elem": neighbour[side]}
        )

    def backward(side):
        return remote(
            adjoint.at[STEPS, :, own_ds[side]], adjoint_in.at[:, own_ds[side]],
            BACKWARD + side, {"sec": other},
        )

    def up(side):
        rows = pl.ds(own_elems[side].start, radius)
        return remote(upper.at[rows], upper_in.at[rows], UPPER + side, {"sec": other})

    @pl.when(section == 0)
    def _():
        halo_copy(0, LEFT).start()
        halo_copy(0, RIGHT).start()

    for e in range(elems):
        jac_loads[e].wait()

        def split_one(d, carry, e=e):
            target = lax.rem(first_elem + e + d - radius + elem_total, elem_total)
            slot = jnp.int32(0)
            for k in range(1, nbrs):
                slot = jnp.where(neighbors[e, k] == target, jnp.int32(k), slot)
            high, low = halves(jac_f32[e][slot])
            lanes = pl.ds(pl.multiple_of(d * order, order), order)
            jac_high[e][:, lanes] = high
            jac_low[e][:, lanes] = low
            return carry

        lax.fori_loop(0, nbrs, split_one, 0)

    weights_load.wait()
    weights_ref[stats:, :] = jnp.zeros((weights_ref.shape[0] - stats, order), F32)
    weights_high, weights_low = halves(weights_ref[...])
    lane_ids = lax.broadcasted_iota(jnp.int32, (cols, LANES), 1)
    station_row = jnp.full((cols, LANES), -1, jnp.int32)
    for i in range(stats):
        station_row = jnp.where(lane_ids == i, stations[i], station_row)

    def receive_forward(core, away):
        @pl.when(section == 1)
        def _():
            forward(core).wait_recv()
            halo_copy(0, core).start()
            forward(away).wait_recv()

    by_parity(receive_forward)

    def put_field(start, value):
        high, low = halves(value)
        field[:cols, start : start + value.shape[1]] = high
        field[cols:, start : start + value.shape[1]] = low

    def blocks(ref, begin, end):
        return ref[:, begin * order : end * order]

    def gathered(e, low, high):
        return product3(
            blocks(field, low, high), blocks(jac_high[e], low - e, high - e),
            blocks(jac_low[e], low - e, high - e), True,
        )

    def here(e):
        return slice(e * order, (e + 1) * order)

    def finish_tangent(t, side, away):
        halo_copy(t, 1 - side).wait_recv()
        put_field(0 if side == LEFT else width + full, halo_in[side][t])
        for e in own_elems[side]:
            span = (e, radius) if side == LEFT else (edge, e + nbrs)
            state[t + 1, :, here(e)] = state[t + 1, :, here(e)] + gathered(e, *span)
        if t < last:
            halo_copy(t + 1, side).start()
        else:

            @pl.when(section == 0)
            def _():
                forward(side).start()
                if away:
                    halo_across(side).start()

    for t in range(STEPS):
        put_field(width, state[t])
        for e in range(elems):
            added = gathered(e, max(e, radius), min(e + nbrs, edge))
            state[t + 1, :, here(e)] = state[t, :, here(e)] + added

        def finish(core, away, t=t):
            finish_tangent(t, core, False)
            finish_tangent(t, away, True)

        by_parity(finish)

    reading = jnp.zeros((cols, LANES), F32)
    for e in range(elems):
        stack = jnp.concatenate(halves(state[STEPS, :, here(e)]), axis=0)
        read = product3(stack, weights_high, weights_low, True)
        read = jnp.where(station_row == first_elem + e, read, 0.0)
        reading = reading + read
        stack = jnp.concatenate(halves(read), axis=0)
        observed[:, here(e)] = product3(stack, weights_high, weights_low, False)
    for slot in range(n_col, readings.shape[0]):
        readings[slot] = jnp.zeros((cols, LANES), F32)
    readings[column] = reading
    read_copies = [
        remote(
            readings.at[column], readings.at[column], READ + j - 1,
            {"col": lax.rem(column + j, n_col)},
        )
        for j in range(1, n_col)
    ]
    for copy in read_copies:
        copy.start()
    gram_copy = remote(partial.at[rounds], partial_in.at[rounds], GRAM, {"sec": other})

    def project():
        for copy in read_copies:
            copy.wait_recv()
        everyone = readings[...].reshape(readings.shape[0] * cols, LANES)
        high, low = halves(everyone)
        stack = jnp.concatenate(halves(readings[column]), axis=0)
        partial[0] = product3(stack, high, low, True)
        for r in range(rounds):
            copy = remote(partial.at[r], partial_in.at[r], FLIP + r, flips[r])
            copy.start()
            copy.wait_recv()
            partial[r + 1] = partial[r] + partial_in[r]
            copy.wait_send()
        gram_copy.start()

    @pl.when(section == 0)
    def _():
        project()

    def spread(e, low, high):
        return product3(
            field[:, here(e)], blocks(jac_high[e], low - e, high - e),
            blocks(jac_low[e], low - e, high - e), False,
        )

    def send_out(t, side, away):
        put_field(own[side].start, adjoint[t, :, own[side]])
        ref = out[side]
        if side == LEFT:
            ref[t] = spread(0, 0, radius)
            for e in range(1, radius):
                ref[t, :, e * order :] = ref[t, :, e * order :] + spread(e, e, radius)
        else:
            ref[t] = spread(elems - 1, edge, edge + radius)
            for e in range(elems - radius, elems - 1):
                size = (e + nbrs - edge) * order
                ref[t, :, :size] = ref[t, :, :size] + spread(e, edge, e + nbrs)
        if t == last and away:

            @pl.when(section == 0)
            def _():
                out_copy(t, side).start()

            @pl.when(section == 1)
            def _():
                out_across(side).start()

        else:
            out_copy(t, side).start()

    def begin_adjoint(core, away):
        for side in (away, core):
            lanes = own[side]

            @pl.when(section == 0)
            def _():
                backward(side).wait_recv()
                total = adjoint_in[:, lanes] + observed[:, lanes]
                if side == away:
                    out_across(1 - side).wait_recv()
                    total = total + back_across[...]
                adjoint[0, :, lanes] = total

            @pl.when(section == 1)
            def _():
                adjoint[0, :, lanes] = observed[:, lanes]

            send_out(0, side, side == away)

    by_parity(begin_adjoint)

    def emit(side):
        for e in own_elems[side]:
            upper[e] = adjoint[STEPS, :, e * order + half : (e + 1) * order]
        up(side).start()
        for e in own_elems[side]:
            hess_ref[e] = adjoint[STEPS, :, e * order : e * order + half]

    def finish_adjoint(t, side, away):
        lanes = own[side]

        def add():
            out_copy(t, 1 - side).wait_recv()
            adjoint[t + 1, :, lanes] = adjoint[t + 1, :, lanes] + back[side][t]

        if t < last:
            add()
            send_out(t + 1, side, away)
        else:

            @pl.when(section == 0)
            def _():
                add()
                emit(side)

            @pl.when(section == 1)
            def _():
                if not away:
                    add()
                backward(side).start()

    for t in range(STEPS):
        adjoint[t + 1] = adjoint[t]
        for e in range(elems):
            low, high = max(e, radius), min(e + nbrs, edge)
            lanes = slice((low - radius) * order, (high - radius) * order)
            adjoint[t + 1, :, lanes] = adjoint[t + 1, :, lanes] + spread(e, low, high)

        def finish(core, away, t=t):
            if t == last:

                @pl.when(section == 1)
                def _():
                    finish_adjoint(t, away, True)
                    finish_adjoint(t, core, False)

                @pl.when(section == 0)
                def _():
                    finish_adjoint(t, core, False)
                    finish_adjoint(t, away, True)

            else:
                finish_adjoint(t, core, False)
                finish_adjoint(t, away, True)

        by_parity(finish)

    @pl.when(section == 1)
    def _():
        project()

    gram_copy.wait_recv()
    scale = 1.0 / (elem_total * order)
    gram_ref[...] = (partial[rounds] + partial_in[rounds]) * scale

    def close(core, away):
        for t in range(STEPS):
            for side in (core, away):

                @pl.when((section == 0) | (t > 0) | (side == core))
                def _():
                    halo_copy(t, side).wait_send()

                @pl.when((section == 0) | (t < last) | (side == core))
                def _():
                    out_copy(t, side).wait_send()

        @pl.when(section == 0)
        def _():
            halo_across(away).wait_send()
            for side in (core, away):
                forward(side).wait_send()
                up(side).wait_send()

        @pl.when(section == 1)
        def _():
            out_across(away).wait_send()
            for side in (core, away):
                backward(side).wait_send()
                up(side).wait_recv()
            hess_ref[...] = upper_in[...]

    by_parity(close)
    gram_copy.wait_send()
    for copy in read_copies:
        copy.wait_send()


def per_device(n_elem, n_col, probes, jacobian, neighbors, stations, obs_weights):
    cols, elems, order = probes.shape
    nbrs = neighbors.shape[1]
    stats = stations.shape[0]
    radius = (nbrs - 1) // 2
    rounds = int(math.log2(n_elem))
    slots = max(n_col, LANES // cols)
    sizes = (cols, elems, order, nbrs, stats, n_elem, n_col)
    full, width = elems * order, radius * order
    copies = 4 * STEPS + 9 + (n_col - 1) + rounds
    scratch = [pltpu.VMEM((nbrs, order, order), F32)] * elems
    scratch += [pltpu.VMEM((order, nbrs * order), BF16)] * (2 * elems)
    scratch += [
        pltpu.VMEM((elems, cols, order), F32),
        pltpu.VMEM((LANES, order), F32),
        pltpu.VMEM((STEPS + 1, cols, full), F32),
        pltpu.VMEM((2 * cols, full + 2 * width), BF16),
        pltpu.VMEM((STEPS, cols, width), F32),
        pltpu.VMEM((STEPS, cols, width), F32),
        pltpu.VMEM((STEPS + 1, cols, full), F32),
        pltpu.VMEM((cols, full), F32),
        pltpu.VMEM((cols, full), F32),
        pltpu.VMEM((STEPS, cols, width), F32),
        pltpu.VMEM((STEPS, cols, width), F32),
        pltpu.VMEM((STEPS, cols, width), F32),
        pltpu.VMEM((STEPS, cols, width), F32),
        pltpu.VMEM((cols, width), F32),
        pltpu.VMEM((slots, cols, LANES), F32),
        pltpu.VMEM((rounds + 1, cols, slots * cols), F32),
        pltpu.VMEM((rounds + 1, cols, slots * cols), F32),
        pltpu.VMEM((elems, cols, order // 2), F32),
        pltpu.VMEM((elems, cols, order // 2), F32),
        pltpu.SemaphoreType.DMA((elems + 2,)),
        pltpu.SemaphoreType.DMA((copies,)),
        pltpu.SemaphoreType.DMA((copies,)),
    ]
    smem = pl.BlockSpec(memory_space=pltpu.SMEM)
    anywhere = pl.BlockSpec(memory_space=pl.ANY)
    vmem = pl.BlockSpec(memory_space=pltpu.VMEM)
    hess, gram = pl.pallas_call(
        functools.partial(kernel, sizes),
        out_shape=(
            jax.ShapeDtypeStruct((elems, cols, order // 2), F32),
            jax.ShapeDtypeStruct((cols, slots * cols), F32),
        ),
        in_specs=[smem, smem, anywhere, anywhere, anywhere],
        out_specs=(vmem, vmem),
        scratch_shapes=scratch,
        compiler_params=pltpu.CompilerParams(
            collective_id=0, has_side_effects=True, vmem_limit_bytes=56 * 1024 * 1024
        ),
    )(neighbors, stations, probes.transpose(1, 0, 2), jacobian, obs_weights)
    return hess.transpose(1, 0, 2), gram[:, : n_col * cols]


def solution(mesh):
    in_specs = (
        P("col", "elem", None),
        P("sec", "elem", None, None, None),
        P("elem", None),
        P("elem"),
        P("elem", None),
    )
    out_specs = (P("col", "elem", "sec"), P("col", None))
    body = functools.partial(per_device, mesh.shape["elem"], mesh.shape["col"])
    return jax.shard_map(
        body, mesh=mesh, in_specs=in_specs, out_specs=out_specs, check_vma=False
    )
```

time: 68.9 us -> 61.5 us (0.89)
  Pallas kernels: 63.3 us -> 57.7 us
  local copies, waits for them, and re-layouts: 4.6 us -> 2.86 us
    pallas_call x1, Pallas kernels: 63.3 us -> 57.7 us  [per_device(): pl.pallas_call(functools.partial(kernel, sizes), out_shape=(jax.ShapeDtyp...]
    unnamed x3 -> x2, local copies, waits for them, and re-layouts: 4.6 us -> 2.86 us
where the time goes in v2:
time: 61.5 us; the launch traced here: 61.2 us
  Pallas kernels  57.7 us (94%)
  local copies, waits for them, and re-layouts  2.86 us (5%)
  between operations  0.64 us (1%)
    pallas_call x1, Pallas kernels, per_device(): pl.pallas_call(functools.partial(kernel, sizes), out_shape=(jax.ShapeDtyp...  57.7 us
    unnamed x2, local copies, waits for them, and re-layouts  2.86 us

profile of v2, /device:TPU:0, one launch (start us, length us, event | category | flops | bytes accessed | tf_op | source)
XLA Modules:
  0.0 61.2 jit_solution(879788957056406039)
XLA Ops:
  0.6 57.7 %shard_map.68 = (f32[6,32,128]{2,1,0:T(8,128)}, f32[32,128]{1,0:T(8,128)}) custom-call(s32[6,7]{1,0:T(8,128)} %neighbors.1, s32[64]{0:T(128)} %stations.1, f32[6,32,256]{2,1,0:T(8,128)} %bitcast.3, f32[1,6,7,256,256]{4,3,2,1,0:T(8,128)} %jacobian_hbm.1, f32[64,256]{1,0:T(8,128)} %weights_hbm.1), custom_call_target="tpu_custom_call" | custom-call | tf_op jit(solution)/shard_map/pallas_call | solution.py:488
  58.3 1.5 %copy.9 = f32[32,6,128]{2,0,1:T(8,128)} copy(f32[32,6,128]{2,0,1:T(8,128)} %bitcast.4) | data formatting | bytes 196608
  59.9 1.3 %copy.10 = f32[32,64]{1,0:T(8,128)} copy(f32[32,64]{1,0:T(8,128)} %bitcast.5) | data formatting | bytes 16384

commit v3 on v2

--- a/solution.py
+++ b/solution.py
@@ -54,7 +54,7 @@
     (
         probes_ref, weights_ref, state, field, halo_left, halo_right,
         adjoint, adjoint_in, observed, out_left, out_right, back_left, back_right,
-        back_across, readings, partial, partial_in, upper, upper_in,
+        back_across, out_half, back_half, readings, partial, partial_in, upper, upper_in,
         load_sem, send_sem, recv_sem,
     ) = scratch[3 * elems :]
     section = lax.axis_index("sec")
@@ -79,6 +79,7 @@
     own = (slice(0, width), slice(full - width, full))
     own_ds = (pl.ds(0, width), pl.ds(full - width, width))
     own_elems = (range(0, radius), range(elems - radius, elems))
+    own_span = ((radius, 2 * radius), (edge - radius, edge))
 
     def by_parity(run):
         @pl.when(even)
@@ -131,7 +132,7 @@
 
     FORWARD = 4 * STEPS
     BACKWARD, UPPER = FORWARD + 2, FORWARD + 4
-    ACROSS, RETURN, GRAM, READ = (FORWARD + 6 + i for i in range(4))
+    ACROSS, RETURN, GRAM, LOWER, HIGHER, READ = (FORWARD + 6 + i for i in range(6))
     FLIP = READ + n_col - 1
 
     def halo_copy(t, side):
@@ -167,6 +168,12 @@
         return remote(
             adjoint.at[STEPS, :, own_ds[side]], adjoint_in.at[:, own_ds[side]],
             BACKWARD + side, {"sec": other},
+        )
+
+    def half_copy(part, side):
+        return remote(
+            out_half.at[part], back_half, (LOWER, HIGHER)[part],
+            {"sec": section if part == 0 else other, "elem": neighbour[side]},
         )
 
     def up(side):
@@ -202,15 +209,6 @@
     for i in range(stats):
         station_row = jnp.where(lane_ids == i, stations[i], station_row)
 
-    def receive_forward(core, away):
-        @pl.when(section == 1)
-        def _():
-            forward(core).wait_recv()
-            halo_copy(0, core).start()
-            forward(away).wait_recv()
-
-    by_parity(receive_forward)
-
     def put_field(start, value):
         high, low = halves(value)
         field[:cols, start : start + value.shape[1]] = high
@@ -244,17 +242,33 @@
                 if away:
                     halo_across(side).start()
 
+    def tangent(t, core, away):
+        if t == 0:
+            for side in (core, away):
+
+                @pl.when(section == 1)
+                def _():
+                    forward(side).wait_recv()
+                    if side == core:
+                        halo_copy(0, core).start()
+
+                put_field(width + own[side].start, state[0, :, own[side]])
+                begin, end = own_span[side]
+                for e in range(elems):
+                    added = gathered(e, max(e, begin), min(e + nbrs, end))
+                    if side == away:
+                        added = added + (state[1, :, here(e)] + state[0, :, here(e)])
+                    state[1, :, here(e)] = added
+        finish_tangent(t, core, False)
+        finish_tangent(t, away, True)
+
     for t in range(STEPS):
-        put_field(width, state[t])
-        for e in range(elems):
-            added = gathered(e, max(e, radius), min(e + nbrs, edge))
-            state[t + 1, :, here(e)] = state[t, :, here(e)] + added
-
-        def finish(core, away, t=t):
-            finish_tangent(t, core, False)
-            finish_tangent(t, away, True)
-
-        by_parity(finish)
+        if t > 0:
+            put_field(width, state[t])
+            for e in range(elems):
+                added = gathered(e, max(e, radius), min(e + nbrs, edge))
+                state[t + 1, :, here(e)] = state[t, :, here(e)] + added
+        by_parity(functools.partial(tangent, t))
 
     reading = jnp.zeros((cols, LANES), F32)
     for e in range(elems):
@@ -319,7 +333,11 @@
 
             @pl.when(section == 0)
             def _():
-                out_copy(t, side).start()
+                for part in range(2):
+                    for j in range(radius):
+                        lanes = slice(j * order + part * half, j * order + (part + 1) * half)
+                        out_half[part, :, j * half : (j + 1) * half] = ref[t, :, lanes]
+                    half_copy(part, side).start()
 
             @pl.when(section == 1)
             def _():
@@ -349,61 +367,65 @@
 
     by_parity(begin_adjoint)
 
-    def emit(side):
+    def inner(t, side):
+        begin, end = own_span[side]
+        lanes = own[side]
+        adjoint[t + 1, :, lanes] = adjoint[t, :, lanes]
+        for e in range(elems):
+            low, high = max(e, begin), min(e + nbrs, end)
+            lanes = slice((low - radius) * order, (high - radius) * order)
+            adjoint[t + 1, :, lanes] = adjoint[t + 1, :, lanes] + spread(e, low, high)
+
+    def add_back(t, side):
+        lanes = own[side]
+        out_copy(t, 1 - side).wait_recv()
+        adjoint[t + 1, :, lanes] = adjoint[t + 1, :, lanes] + back[side][t]
+
+    def send_up(side):
         for e in own_elems[side]:
             upper[e] = adjoint[STEPS, :, e * order + half : (e + 1) * order]
         up(side).start()
-        for e in own_elems[side]:
-            hess_ref[e] = adjoint[STEPS, :, e * order : e * order + half]
-
-    def finish_adjoint(t, side, away):
-        lanes = own[side]
-
-        def add():
-            out_copy(t, 1 - side).wait_recv()
-            adjoint[t + 1, :, lanes] = adjoint[t + 1, :, lanes] + back[side][t]
-
+
+    def lower_half(e):
+        return adjoint[STEPS, :, e * order : e * order + half]
+
+    def adjoint_step(t, core, away):
         if t < last:
-            add()
-            send_out(t + 1, side, away)
+            for side in (core, away):
+                add_back(t, side)
+                send_out(t + 1, side, side == away)
         else:
+            inner(t, away)
 
             @pl.when(section == 0)
             def _():
-                add()
-                emit(side)
+                send_up(away)
 
             @pl.when(section == 1)
             def _():
-                if not away:
-                    add()
-                backward(side).start()
+                backward(away).start()
+
+            inner(t, core)
+            add_back(t, core)
+
+            @pl.when(section == 0)
+            def _():
+                send_up(core)
+                for e in own_elems[core]:
+                    hess_ref[e] = lower_half(e)
+                half_copy(0, 1 - away).wait_recv()
+                for j, e in enumerate(own_elems[away]):
+                    hess_ref[e] = lower_half(e) + back_half[:, j * half : (j + 1) * half]
+
+            @pl.when(section == 1)
+            def _():
+                backward(core).start()
 
     for t in range(STEPS):
-        adjoint[t + 1] = adjoint[t]
-        for e in range(elems):
-            low, high = max(e, radius), min(e + nbrs, edge)
-            lanes = slice((low - radius) * order, (high - radius) * order)
-            adjoint[t + 1, :, lanes] = adjoint[t + 1, :, lanes] + spread(e, low, high)
-
-        def finish(core, away, t=t):
-            if t == last:
-
-                @pl.when(section == 1)
-                def _():
-                    finish_adjoint(t, away, True)
-                    finish_adjoint(t, core, False)
-
-                @pl.when(section == 0)
-                def _():
-                    finish_adjoint(t, core, False)
-                    finish_adjoint(t, away, True)
-
-            else:
-                finish_adjoint(t, core, False)
-                finish_adjoint(t, away, True)
-
-        by_parity(finish)
+        if t < last:
+            inner(t, LEFT)
+            inner(t, RIGHT)
+        by_parity(functools.partial(adjoint_step, t))
 
     @pl.when(section == 1)
     def _():
@@ -421,8 +443,7 @@
                 def _():
                     halo_copy(t, side).wait_send()
 
-                @pl.when((section == 0) | (t < last) | (side == core))
-                def _():
+                if t < last or side == core:
                     out_copy(t, side).wait_send()
 
         @pl.when(section == 0)
@@ -431,6 +452,8 @@
             for side in (core, away):
                 forward(side).wait_send()
                 up(side).wait_send()
+            for part in range(2):
+                half_copy(part, away).wait_send()
 
         @pl.when(section == 1)
         def _():
@@ -438,12 +461,21 @@
             for side in (core, away):
                 backward(side).wait_send()
                 up(side).wait_recv()
-            hess_ref[...] = upper_in[...]
+            for e in own_elems[core]:
+                hess_ref[e] = upper_in[e]
+            half_copy(1, 1 - away).wait_recv()
+            for j, e in enumerate(own_elems[away]):
+                hess_ref[e] = upper_in[e] + back_half[:, j * half : (j + 1) * half]
 
     by_parity(close)
     gram_copy.wait_send()
     for copy in read_copies:
         copy.wait_send()
+
+
+def hand_over(hess_ref, gram_ref, hess_out, gram_out):
+    hess_out[...] = hess_ref[...]
+    gram_out[...] = gram_ref[:, : gram_out.shape[1]]
 
 
 def per_device(n_elem, n_col, probes, jacobian, neighbors, stations, obs_weights):
@@ -455,7 +487,7 @@
     slots = max(n_col, LANES // cols)
     sizes = (cols, elems, order, nbrs, stats, n_elem, n_col)
     full, width = elems * order, radius * order
-    copies = 4 * STEPS + 9 + (n_col - 1) + rounds
+    copies = 4 * STEPS + 11 + (n_col - 1) + rounds
     scratch = [pltpu.VMEM((nbrs, order, order), F32)] * elems
     scratch += [pltpu.VMEM((order, nbrs * order), BF16)] * (2 * elems)
     scratch += [
@@ -473,6 +505,8 @@
         pltpu.VMEM((STEPS, cols, width), F32),
         pltpu.VMEM((STEPS, cols, width), F32),
         pltpu.VMEM((cols, width), F32),
+        pltpu.VMEM((2, cols, width // 2), F32),
+        pltpu.VMEM((cols, width // 2), F32),
         pltpu.VMEM((slots, cols, LANES), F32),
         pltpu.VMEM((rounds + 1, cols, slots * cols), F32),
         pltpu.VMEM((rounds + 1, cols, slots * cols), F32),
@@ -498,7 +532,16 @@
             collective_id=0, has_side_effects=True, vmem_limit_bytes=56 * 1024 * 1024
         ),
     )(neighbors, stations, probes.transpose(1, 0, 2), jacobian, obs_weights)
-    return hess.transpose(1, 0, 2), gram[:, : n_col * cols]
+    hess, gram = pl.pallas_call(
+        hand_over,
+        out_shape=(
+            jax.ShapeDtypeStruct(hess.shape, F32),
+            jax.ShapeDtypeStruct((cols, n_col * cols), F32),
+        ),
+        in_specs=[vmem, vmem],
+        out_specs=(vmem, vmem),
+    )(hess, gram)
+    return hess.transpose(1, 0, 2), gram
 
 
 def solution(mesh):

time: 61.5 us -> 56.7 us (0.922)
  local copies, waits for them, and re-layouts: 2.86 us -> 0 us
  Pallas kernels: 57.7 us -> 55.9 us
    pallas_call x1, Pallas kernels: 57.7 us -> 54.3 us  [per_device(): pl.pallas_call(functools.partial(kernel, sizes), out_shape=(jax.ShapeDtyp...]
    unnamed x2 -> x0, local copies, waits for them, and re-layouts: 2.86 us -> none
    pallas_call x0 -> x1, Pallas kernels: none -> 1.55 us  [per_device(): pl.pallas_call(hand_over, out_shape=(jax.ShapeDtypeStruct(hess.shape, F32...]
where the time goes in v3:
time: 56.7 us; the launch traced here: 56.5 us
  Pallas kernels  55.9 us (99%)
  between operations  0.64 us (1%)
    pallas_call x1, Pallas kernels, per_device(): pl.pallas_call(functools.partial(kernel, sizes), out_shape=(jax.ShapeDtyp...  54.3 us
    pallas_call x1, Pallas kernels, per_device(): pl.pallas_call(hand_over, out_shape=(jax.ShapeDtypeStruct(hess.shape, F32...  1.55 us

profile of v3, /device:TPU:0, one launch (start us, length us, event | category | flops | bytes accessed | tf_op | source)
XLA Modules:
  0.0 56.5 jit_solution(10026493238071927582)
XLA Ops:
  0.6 54.3 %shard_map.68 = (f32[6,32,128]{2,1,0:T(8,128)}, f32[32,128]{1,0:T(8,128)}) custom-call(s32[6,7]{1,0:T(8,128)} %neighbors.1, s32[64]{0:T(128)} %stations.1, f32[6,32,256]{2,1,0:T(8,128)} %bitcast.2, f32[1,6,7,256,256]{4,3,2,1,0:T(8,128)} %jacobian_hbm.1, f32[64,256]{1,0:T(8,128)} %weights_hbm.1), custom_call_target="tpu_custom_call" | custom-call | tf_op jit(solution)/shard_map/pallas_call | solution.py:522
  55.0 1.5 %shard_map.69 = (f32[6,32,128]{2,1,0:T(8,128)}, f32[32,64]{1,0:T(8,128)}) custom-call(f32[6,32,128]{2,1,0:T(8,128)} %get-tuple-element.6.hess_ref, f32[32,128]{1,0:T(8,128)} %get-tuple-element.7.gram_ref), custom_call_target="tpu_custom_call" | custom-call | tf_op jit(solution)/shard_map/pallas_call | solution.py:535

commit v4 on v3

--- a/solution.py
+++ b/solution.py
@@ -185,21 +185,57 @@
         halo_copy(0, LEFT).start()
         halo_copy(0, RIGHT).start()
 
-    for e in range(elems):
-        jac_loads[e].wait()
-
-        def split_one(d, carry, e=e):
-            target = lax.rem(first_elem + e + d - radius + elem_total, elem_total)
-            slot = jnp.int32(0)
-            for k in range(1, nbrs):
-                slot = jnp.where(neighbors[e, k] == target, jnp.int32(k), slot)
-            high, low = halves(jac_f32[e][slot])
-            lanes = pl.ds(pl.multiple_of(d * order, order), order)
-            jac_high[e][:, lanes] = high
-            jac_low[e][:, lanes] = low
-            return carry
-
-        lax.fori_loop(0, nbrs, split_one, 0)
+    def put_field(start, value):
+        high, low = halves(value)
+        field[:cols, start : start + value.shape[1]] = high
+        field[cols:, start : start + value.shape[1]] = low
+
+    def blocks(ref, begin, end):
+        return ref[:, begin * order : end * order]
+
+    def gathered(e, low, high):
+        return product3(
+            blocks(field, low, high), blocks(jac_high[e], low - e, high - e),
+            blocks(jac_low[e], low - e, high - e), True,
+        )
+
+    def here(e):
+        return slice(e * order, (e + 1) * order)
+
+    def split(e, d, lanes):
+        target = lax.rem(first_elem + e + d - radius + elem_total, elem_total)
+        slot = jnp.int32(0)
+        for k in range(1, nbrs):
+            slot = jnp.where(neighbors[e, k] == target, jnp.int32(k), slot)
+        high, low = halves(jac_f32[e][slot])
+        jac_high[e][:, lanes] = high
+        jac_low[e][:, lanes] = low
+
+    def inner_tangent(t, e):
+        added = gathered(e, max(e, radius), min(e + nbrs, edge))
+        state[t + 1, :, here(e)] = state[t, :, here(e)] + added
+
+    @pl.when(section == 0)
+    def _():
+        put_field(width, state[0])
+        for e in range(elems):
+            jac_loads[e].wait()
+            for d in range(nbrs):
+                split(e, d, here(d))
+            if e > 0:
+                inner_tangent(0, e - 1)
+        inner_tangent(0, elems - 1)
+
+    @pl.when(section == 1)
+    def _():
+        for e in range(elems):
+            jac_loads[e].wait()
+
+            def split_one(d, carry, e=e):
+                split(e, d, pl.ds(pl.multiple_of(d * order, order), order))
+                return carry
+
+            lax.fori_loop(0, nbrs, split_one, 0)
 
     weights_load.wait()
     weights_ref[stats:, :] = jnp.zeros((weights_ref.shape[0] - stats, order), F32)
@@ -208,23 +244,6 @@
     station_row = jnp.full((cols, LANES), -1, jnp.int32)
     for i in range(stats):
         station_row = jnp.where(lane_ids == i, stations[i], station_row)
-
-    def put_field(start, value):
-        high, low = halves(value)
-        field[:cols, start : start + value.shape[1]] = high
-        field[cols:, start : start + value.shape[1]] = low
-
-    def blocks(ref, begin, end):
-        return ref[:, begin * order : end * order]
-
-    def gathered(e, low, high):
-        return product3(
-            blocks(field, low, high), blocks(jac_high[e], low - e, high - e),
-            blocks(jac_low[e], low - e, high - e), True,
-        )
-
-    def here(e):
-        return slice(e * order, (e + 1) * order)
 
     def finish_tangent(t, side, away):
         halo_copy(t, 1 - side).wait_recv()
@@ -244,21 +263,21 @@
 
     def tangent(t, core, away):
         if t == 0:
-            for side in (core, away):
-
-                @pl.when(section == 1)
-                def _():
+
+            @pl.when(section == 1)
+            def _():
+                for side in (core, away):
                     forward(side).wait_recv()
                     if side == core:
                         halo_copy(0, core).start()
-
-                put_field(width + own[side].start, state[0, :, own[side]])
-                begin, end = own_span[side]
-                for e in range(elems):
-                    added = gathered(e, max(e, begin), min(e + nbrs, end))
-                    if side == away:
-                        added = added + (state[1, :, here(e)] + state[0, :, here(e)])
-                    state[1, :, here(e)] = added
+                    put_field(width + own[side].start, state[0, :, own[side]])
+                    begin, end = own_span[side]
+                    for e in range(elems):
+                        added = gathered(e, max(e, begin), min(e + nbrs, end))
+                        if side == away:
+                            added = added + (state[1, :, here(e)] + state[0, :, here(e)])
+                        state[1, :, here(e)] = added
+
         finish_tangent(t, core, False)
         finish_tangent(t, away, True)
 
@@ -266,8 +285,7 @@
         if t > 0:
             put_field(width, state[t])
             for e in range(elems):
-                added = gathered(e, max(e, radius), min(e + nbrs, edge))
-                state[t + 1, :, here(e)] = state[t, :, here(e)] + added
+                inner_tangent(t, e)
         by_parity(functools.partial(tangent, t))
 
     reading = jnp.zeros((cols, LANES), F32)
@@ -292,16 +310,23 @@
         copy.start()
     gram_copy = remote(partial.at[rounds], partial_in.at[rounds], GRAM, {"sec": other})
 
-    def project():
+    def project_start():
         for copy in read_copies:
             copy.wait_recv()
         everyone = readings[...].reshape(readings.shape[0] * cols, LANES)
         high, low = halves(everyone)
         stack = jnp.concatenate(halves(readings[column]), axis=0)
         partial[0] = product3(stack, high, low, True)
+        flip_copy(0).start()
+
+    def flip_copy(r):
+        return remote(partial.at[r], partial_in.at[r], FLIP + r, flips[r])
+
+    def project_finish():
         for r in range(rounds):
-            copy = remote(partial.at[r], partial_in.at[r], FLIP + r, flips[r])
-            copy.start()
+            copy = flip_copy(r)
+            if r > 0:
+                copy.start()
             copy.wait_recv()
             partial[r + 1] = partial[r] + partial_in[r]
             copy.wait_send()
@@ -309,7 +334,8 @@
 
     @pl.when(section == 0)
     def _():
-        project()
+        project_start()
+        project_finish()
 
     def spread(e, low, high):
         return product3(
@@ -425,11 +451,17 @@
         if t < last:
             inner(t, LEFT)
             inner(t, RIGHT)
+        if t == 0:
+
+            @pl.when(section == 1)
+            def _():
+                project_start()
+
         by_parity(functools.partial(adjoint_step, t))
 
     @pl.when(section == 1)
     def _():
-        project()
+        project_finish()
 
     gram_copy.wait_recv()
     scale = 1.0 / (elem_total * order)

time: 56.7 us -> 58 us (1.023)
  Pallas kernels: 55.9 us -> 57.1 us
    pallas_call x1, Pallas kernels: 54.3 us -> 55.6 us  [per_device(): pl.pallas_call(functools.partial(kernel, sizes), out_shape=(jax.ShapeDtyp...]
where the time goes in v4:
time: 58 us; the launch traced here: 57.8 us
  Pallas kernels  57.1 us (98%)
  between operations  0.64 us (1%)
    pallas_call x1, Pallas kernels, per_device(): pl.pallas_call(functools.partial(kernel, sizes), out_shape=(jax.ShapeDtyp...  55.6 us
    pallas_call x1, Pallas kernels, per_device(): pl.pallas_call(hand_over, out_shape=(jax.ShapeDtypeStruct(hess.shape, F32...  1.55 us

profile of v4, /device:TPU:0, one launch (start us, length us, event | category | flops | bytes accessed | tf_op | source)
XLA Modules:
  0.0 57.8 jit_solution(818401105213798352)
XLA Ops:
  0.6 55.6 %shard_map.68 = (f32[6,32,128]{2,1,0:T(8,128)}, f32[32,128]{1,0:T(8,128)}) custom-call(s32[6,7]{1,0:T(8,128)} %neighbors.1, s32[64]{0:T(128)} %stations.1, f32[6,32,256]{2,1,0:T(8,128)} %bitcast.2, f32[1,6,7,256,256]{4,3,2,1,0:T(8,128)} %jacobian_hbm.1, f32[64,256]{1,0:T(8,128)} %weights_hbm.1), custom_call_target="tpu_custom_call" | custom-call | tf_op jit(solution)/shard_map/pallas_call | solution.py:554
  56.2 1.5 %shard_map.69 = (f32[6,32,128]{2,1,0:T(8,128)}, f32[32,64]{1,0:T(8,128)}) custom-call(f32[6,32,128]{2,1,0:T(8,128)} %get-tuple-element.6.hess_ref, f32[32,128]{1,0:T(8,128)} %get-tuple-element.7.gram_ref), custom_call_target="tpu_custom_call" | custom-call | tf_op jit(solution)/shard_map/pallas_call | solution.py:567

commit v5 on v4

--- a/solution.py
+++ b/solution.py
@@ -218,24 +218,19 @@
     @pl.when(section == 0)
     def _():
         put_field(width, state[0])
-        for e in range(elems):
-            jac_loads[e].wait()
-            for d in range(nbrs):
-                split(e, d, here(d))
-            if e > 0:
-                inner_tangent(0, e - 1)
-        inner_tangent(0, elems - 1)
-
-    @pl.when(section == 1)
-    def _():
-        for e in range(elems):
-            jac_loads[e].wait()
-
-            def split_one(d, carry, e=e):
-                split(e, d, pl.ds(pl.multiple_of(d * order, order), order))
-                return carry
-
-            lax.fori_loop(0, nbrs, split_one, 0)
+
+    for e in range(elems):
+        jac_loads[e].wait()
+
+        def split_one(d, carry, e=e):
+            split(e, d, pl.ds(pl.multiple_of(d * order, order), order))
+            return carry
+
+        lax.fori_loop(0, nbrs, split_one, 0)
+
+        @pl.when(section == 0)
+        def _():
+            inner_tangent(0, e)
 
     weights_load.wait()
     weights_ref[stats:, :] = jnp.zeros((weights_ref.shape[0] - stats, order), F32)

time: 58 us -> 57.2 us (0.986)
  Pallas kernels: 57.1 us -> 56.3 us
    pallas_call x1, Pallas kernels: 55.6 us -> 54.8 us  [per_device(): pl.pallas_call(functools.partial(kernel, sizes), out_shape=(jax.ShapeDtyp...]
where the time goes in v5:
time: 57.2 us; the launch traced here: 57 us
  Pallas kernels  56.3 us (98%)
  between operations  0.64 us (1%)
    pallas_call x1, Pallas kernels, per_device(): pl.pallas_call(functools.partial(kernel, sizes), out_shape=(jax.ShapeDtyp...  54.8 us
    pallas_call x1, Pallas kernels, per_device(): pl.pallas_call(hand_over, out_shape=(jax.ShapeDtypeStruct(hess.shape, F32...  1.55 us

profile of v5, /device:TPU:0, one launch (start us, length us, event | category | flops | bytes accessed | tf_op | source)
XLA Modules:
  0.0 57.0 jit_solution(11363104504885680545)
XLA Ops:
  0.6 54.8 %shard_map.68 = (f32[6,32,128]{2,1,0:T(8,128)}, f32[32,128]{1,0:T(8,128)}) custom-call(s32[6,7]{1,0:T(8,128)} %neighbors.1, s32[64]{0:T(128)} %stations.1, f32[6,32,256]{2,1,0:T(8,128)} %bitcast.2, f32[1,6,7,256,256]{4,3,2,1,0:T(8,128)} %jacobian_hbm.1, f32[64,256]{1,0:T(8,128)} %weights_hbm.1), custom_call_target="tpu_custom_call" | custom-call | tf_op jit(solution)/shard_map/pallas_call | solution.py:549
  55.4 1.5 %shard_map.69 = (f32[6,32,128]{2,1,0:T(8,128)}, f32[32,64]{1,0:T(8,128)}) custom-call(f32[6,32,128]{2,1,0:T(8,128)} %get-tuple-element.6.hess_ref, f32[32,128]{1,0:T(8,128)} %get-tuple-element.7.gram_ref), custom_call_target="tpu_custom_call" | custom-call | tf_op jit(solution)/shard_map/pallas_call | solution.py:562

commit v6 on v3

--- a/solution.py
+++ b/solution.py
@@ -292,16 +292,23 @@
         copy.start()
     gram_copy = remote(partial.at[rounds], partial_in.at[rounds], GRAM, {"sec": other})
 
-    def project():
+    def project_start():
         for copy in read_copies:
             copy.wait_recv()
         everyone = readings[...].reshape(readings.shape[0] * cols, LANES)
         high, low = halves(everyone)
         stack = jnp.concatenate(halves(readings[column]), axis=0)
         partial[0] = product3(stack, high, low, True)
+        flip_copy(0).start()
+
+    def flip_copy(r):
+        return remote(partial.at[r], partial_in.at[r], FLIP + r, flips[r])
+
+    def project_finish():
         for r in range(rounds):
-            copy = remote(partial.at[r], partial_in.at[r], FLIP + r, flips[r])
-            copy.start()
+            copy = flip_copy(r)
+            if r > 0:
+                copy.start()
             copy.wait_recv()
             partial[r + 1] = partial[r] + partial_in[r]
             copy.wait_send()
@@ -309,7 +316,8 @@
 
     @pl.when(section == 0)
     def _():
-        project()
+        project_start()
+        project_finish()
 
     def spread(e, low, high):
         return product3(
@@ -425,11 +433,17 @@
         if t < last:
             inner(t, LEFT)
             inner(t, RIGHT)
+        if t == 0:
+
+            @pl.when(section == 1)
+            def _():
+                project_start()
+
         by_parity(functools.partial(adjoint_step, t))
 
     @pl.when(section == 1)
     def _():
-        project()
+        project_finish()
 
     gram_copy.wait_recv()
     scale = 1.0 / (elem_total * order)

time: 56.7 us -> 56.7 us (level)
  no operation moved by 1% of the time
where the time goes in v6:
time: 56.7 us; the launch traced here: 56.5 us
  Pallas kernels  55.9 us (99%)
  between operations  0.64 us (1%)
    pallas_call x1, Pallas kernels, per_device(): pl.pallas_call(functools.partial(kernel, sizes), out_shape=(jax.ShapeDtyp...  54.3 us
    pallas_call x1, Pallas kernels, per_device(): pl.pallas_call(hand_over, out_shape=(jax.ShapeDtypeStruct(hess.shape, F32...  1.55 us

profile of v6, /device:TPU:0, one launch (start us, length us, event | category | flops | bytes accessed | tf_op | source)
XLA Modules:
  0.0 56.5 jit_solution(18124984925933211136)
XLA Ops:
  0.6 54.3 %shard_map.68 = (f32[6,32,128]{2,1,0:T(8,128)}, f32[32,128]{1,0:T(8,128)}) custom-call(s32[6,7]{1,0:T(8,128)} %neighbors.1, s32[64]{0:T(128)} %stations.1, f32[6,32,256]{2,1,0:T(8,128)} %bitcast.2, f32[1,6,7,256,256]{4,3,2,1,0:T(8,128)} %jacobian_hbm.1, f32[64,256]{1,0:T(8,128)} %weights_hbm.1), custom_call_target="tpu_custom_call" | custom-call | tf_op jit(solution)/shard_map/pallas_call | solution.py:536
  55.0 1.5 %shard_map.69 = (f32[6,32,128]{2,1,0:T(8,128)}, f32[32,64]{1,0:T(8,128)}) custom-call(f32[6,32,128]{2,1,0:T(8,128)} %get-tuple-element.6.hess_ref, f32[32,128]{1,0:T(8,128)} %get-tuple-element.7.gram_ref), custom_call_target="tpu_custom_call" | custom-call | tf_op jit(solution)/shard_map/pallas_call | solution.py:549
